TPU v7x, 512 devices: a whole 4x8x8 slice. The times are simulated.
512 devices in a mesh: ctx: 64 (over x, z_lo, y), head: 8 (over z_hi, core).
Axes of the slice: x: 4, y: 8, z: 8 (z_hi: 4, z_lo: 2; z = z_hi * 2 + z_lo), core: 2. Of those that a mesh axis runs over, the one named last changes fastest.
Arguments:
- queries: bfloat16 [8192, 4096], P(('ctx', 'head')), may hold values from -30 to 30
- keys: bfloat16 [8192, 1024], P(('ctx', 'head')), may hold values from -6 to 6
- values: bfloat16 [8192, 1024], P(('ctx', 'head')), may hold values from -6 to 6
- outputs: bfloat16 [8192, 4096], P(('ctx', 'head')), may hold values from -6 to 6
- output_gradient: bfloat16 [8192, 4096], P(('ctx', 'head')), may hold values from -6 to 6
- importance: int32 [8192], P('ctx'), may hold values from 0 to 8
- span_order: int32 [128], replicated, may hold values from 0 to 127, each once
Outputs:
- query_grad: bfloat16 [8192, 4096], P(('ctx', 'head'))
- key_gradient: bfloat16 [8192, 1024], P(('ctx', 'head'))
- value_gradient: bfloat16 [8192, 1024], P(('ctx', 'head'))
All inputs are finite; a program needn't handle non-finite values.
Results may differ from a plain program's by a relative error of at most 0.0049.
Values may be sent and summed in bfloat16 or wider, within the bound.
A program may use at most 64 MiB of HBM per device.

v0:
```python
import math

import jax
import jax.numpy as jnp
from jax import lax
from jax.sharding import PartitionSpec as P

QUERY_HEADS = 32
KEY_VALUE_HEADS = 8
HEAD_WIDTH = 128
CH = 64


very_low = -1e30


def shifted(array, axis, by):
    size = lax.axis_size(axis)
    return lax.ppermute(array, axis, [(i, (i + by) % size) for i in range(size)])


def key_positions(span_order):
    span_count = span_order.shape[0]
    token_index = jnp.arange(span_count * CH, dtype=jnp.int32)
    span_index = token_index // CH
    matches = span_index[:, None] == jnp.arange(span_count, dtype=jnp.int32)[None, :]
    return jnp.sum(jnp.where(matches, span_order[None, :], 0), axis=1) * CH + token_index % CH


def block_split(length):
    if length > 512 and length % 512 == 0:
        return (512, length // 512)
    return (length, 1)


def on_device(queries, keys, values, outputs, output_gradient, importance, span_order):
    query_loc, output_loc, grad_loc, key_loc, value_loc = (
        lax.all_to_all(queries, "head", split_axis=1, concat_axis=0, tiled=True),
        lax.all_to_all(outputs, "head", split_axis=1, concat_axis=0, tiled=True),
        lax.all_to_all(output_gradient, "head", split_axis=1, concat_axis=0, tiled=True),
        lax.all_to_all(keys, "head", split_axis=1, concat_axis=0, tiled=True),
        lax.all_to_all(values, "head", split_axis=1, concat_axis=0, tiled=True),
    )
    row_count = query_loc.shape[0]
    kv_local = key_loc.shape[1] // HEAD_WIDTH
    group_width = QUERY_HEADS // KEY_VALUE_HEADS
    score_scale = 1.0 / math.sqrt(HEAD_WIDTH)
    cycle_count = lax.axis_size("ctx")
    my_index = lax.axis_index("ctx")
    heads_of_queries = query_loc.reshape(row_count, kv_local, group_width, HEAD_WIDTH)
    gradient_heads = grad_loc.reshape(row_count, kv_local, group_width, HEAD_WIDTH)
    output_heads = output_loc.reshape(row_count, kv_local, group_width, HEAD_WIDTH)
    out_dot = jnp.sum(
        gradient_heads.astype(jnp.float32) * output_heads.astype(jnp.float32), axis=-1
    )
    all_positions = key_positions(span_order)
    query_pos = lax.dynamic_slice_in_dim(all_positions, my_index * row_count, row_count)
    token_gain = importance.astype(jnp.float32) * 0.25
    grad_scale = (token_gain * score_scale)[:, None, None, None]
    gain_wide = token_gain[:, None, None, None]

    def scores_of(key_block, key_pos):
        key_split = key_block.reshape(key_block.shape[0], kv_local, HEAD_WIDTH)
        raw_scores = (
            jnp.einsum(
                "rcgd,ncd->rcgn", heads_of_queries, key_split, preferred_element_type=jnp.float32
            )
            * score_scale
        )
        visible = key_pos[None, None, None, :] <= query_pos[:, None, None, None]
        return (key_split, raw_scores, visible)

    def stats_block(running, inputs):
        key_split, raw_scores, visible = scores_of(inputs[0], inputs[1])
        masked = jnp.where(visible, raw_scores, very_low)
        running_max = jnp.maximum(running[0], jnp.max(masked, axis=-1))
        denominator = running[1] * jnp.exp(running[0] - running_max) + jnp.sum(
            jnp.where(visible, jnp.exp(masked - running_max[..., None]), 0.0), axis=-1
        )
        return ((running_max, denominator), None)

    def grads_block(log_norm, key_block, value_block, key_pos):
        key_split, raw_scores, visible = scores_of(key_block, key_pos)
        value_split = value_block.reshape(value_block.shape[0], kv_local, HEAD_WIDTH)
        probs = jnp.where(visible, jnp.exp(raw_scores - log_norm[..., None]), 0.0)
        prob_grads = jnp.einsum(
            "rcgd,ncd->rcgn", gradient_heads, value_split, preferred_element_type=jnp.float32
        )
        score_grads = (probs * (prob_grads - out_dot[..., None]) * grad_scale).astype(jnp.bfloat16)
        weighted = (probs * gain_wide).astype(jnp.bfloat16)
        query_term = jnp.einsum(
            "rcgn,ncd->rcgd", score_grads, key_split, preferred_element_type=jnp.float32
        )
        key_term = jnp.einsum(
            "rcgn,rcgd->ncd", score_grads, heads_of_queries, preferred_element_type=jnp.float32
        )
        value_term = jnp.einsum(
            "rcgn,rcgd->ncd", weighted, gradient_heads, preferred_element_type=jnp.float32
        )
        length = key_block.shape[0]
        return (
            query_term,
            jnp.concatenate([key_term.reshape(length, -1), value_term.reshape(length, -1)], axis=1),
        )

    def grads_over(log_norm, query_start, key_portion, value_portion, offset):
        length = key_portion.shape[0]
        block_len, block_count = block_split(length)
        key_pos = lax.dynamic_slice_in_dim(all_positions, offset, length)

        def one_block(query_sum, inputs):
            query_term, pair_term = grads_block(log_norm, inputs[0], inputs[1], inputs[2])
            return (query_sum + query_term, pair_term)

        query_sum, pair_terms = lax.scan(
            one_block,
            query_start,
            (
                key_portion.reshape(block_count, block_len, -1),
                value_portion.reshape(block_count, block_len, -1),
                key_pos.reshape(block_count, block_len),
            ),
        )
        return (query_sum, pair_terms.reshape(length, -1))

    stats_start = (
        jnp.full((row_count, kv_local, group_width), very_low, jnp.float32),
        jnp.zeros((row_count, kv_local, group_width), jnp.float32),
    )
    query_zero = jnp.zeros((row_count, kv_local, group_width, HEAD_WIDTH), jnp.float32)
    pair_zero = jnp.zeros((row_count, 2 * kv_local * HEAD_WIDTH), jnp.float32)
    running = stats_start
    portion = lax.all_gather(key_loc, "ctx", axis=0, tiled=True)
    length = portion.shape[0]
    block_len, block_count = block_split(length)
    key_pos = all_positions
    running, unused = lax.scan(
        stats_block,
        running,
        (portion.reshape(block_count, block_len, -1), key_pos.reshape(block_count, block_len)),
    )
    running_max, denominator = running
    log_norm = running_max + jnp.log(denominator)

    def cycle_step(step, carry):
        key_block, value_block, pair_acc, query_sum = carry
        anchor = (my_index - step + cycle_count) % cycle_count
        offset = anchor * row_count
        query_sum, pair_terms = grads_over(log_norm, query_sum, key_block, value_block, offset)
        key_block, value_block = shifted((key_block, value_block), "ctx", 1)
        pair_acc = shifted(pair_acc + pair_terms, "ctx", 1)
        return (key_block, value_block, pair_acc, query_sum)

    unused_keys, unused_values, pair_share, query_sum = lax.fori_loop(
        0, cycle_count, cycle_step, (key_loc, value_loc, pair_zero, query_zero)
    )
    key_width = kv_local * HEAD_WIDTH
    query_part = query_sum.reshape(row_count, -1).astype(jnp.bfloat16)
    key_part = pair_share[:, :key_width].astype(jnp.bfloat16)
    value_part = pair_share[:, key_width:].astype(jnp.bfloat16)
    return (
        lax.all_to_all(query_part, "head", split_axis=0, concat_axis=1, tiled=True),
        lax.all_to_all(key_part, "head", split_axis=0, concat_axis=1, tiled=True),
        lax.all_to_all(value_part, "head", split_axis=0, concat_axis=1, tiled=True),
    )


def solution(mesh):
    in_specs = (
        P(("ctx", "head"), None),
        P(("ctx", "head"), None),
        P(("ctx", "head"), None),
        P(("ctx", "head"), None),
        P(("ctx", "head"), None),
        P("ctx"),
        P(),
    )
    out_specs = (P(("ctx", "head"), None), P(("ctx", "head"), None), P(("ctx", "head"), None))
    return jax.shard_map(
        on_device, mesh=mesh, in_specs=in_specs, out_specs=out_specs, check_vma=False
    )
```

profile of v0, /device:TPU:1, one launch (start us, length us, event | category | flops | bytes accessed | tf_op | source)
XLA Modules:
  0.0 1430.9 jit_solution(9999002778378512729)
XLA Ops:
  7.9 19.0 %all_to_all.137 = bf16[16,8,128]{2,0,1:T(8,128)(2,1)} all-to-all(bf16[16,8,128]{2,0,1:T(8,128)(2,1)S(1)} %copy_bitcast_fusion.6), channel_id=1, replica_groups=mesh['ctx'=64,'head'=8] {'head'}, dimensions={1} | all-to-all | bytes 65536 | tf_op jit(solution)/shard_map/all_to_all | solution.py:41
  28.5 4.0 all-to-all-start.2
  40.6 5.0 all-to-all-start.3
  47.2 7.1 all-to-all-done.3
  54.3 4.4 all-to-all-start.4
  60.3 7.5 all-to-all-done.4
  67.8 4.2 all-to-all-start.1
  72.5 207.1 %all-gather.2.cloned.1.call-done = bf16[8192,128]{1,0:T(8,128)(2,1)} async-done(((bf16[128,128]{1,0:T(8,128)(2,1)}), bf16[8192,128]{1,0:T(8,128)(2,1)}) %all-gather.2.cloned.1.call-update) | async-done | bytes 2097168 | tf_op jit(solution)/shard_map/all_gather | solution.py:133
  279.6 26.5 %while.46 = (s32[]{:T(128)}, f32[128,1,4]{0,2,1:T(4,128)S(1)}, f32[128,1,4]{0,2,1:T(4,128)S(1)}, s32[16,512]{1,0:T(8,128)S(1)}, s32[128]{0:T(128)S(1)}, /*index=...) while((s32[]{:T(128)}, f32[128,1,4]{0,2,1:T(4,128)S(1)}, ...), condition=%wide.region_4.5_spmd.clone, body=%wide.region_1.4_spmd.clone.sunk | while | flops 68749824 | bytes 2589804 | solution.py:137
  306.1 964.0 %while.47 = (s32[]{:T(128)}, bf16[128,128]{1,0:T(8,128)(2,1)S(1)}, bf16[128,128]{1,0:T(8,128)(2,1)S(1)}, f32[128,256]{0,1:T(8,128)S(1)}, f32[128,1,4,128]{3,0,2,...) while((s32[]{:T(128)}, bf16[128,128]{1,0:T(8,128)(2,1)S(1)}, ...), condition=%wide.region_7.8_spmd.clone, body=%wide.region_6.7_spmd.clone.sunk | while | flops 84688912 | bytes 3808750 | solution.py:154
  317.1 4.5 collective-permute-done.2
  332.5 4.0 collective-permute-done.2
  362.1 4.5 collective-permute-done.2
  377.3 4.3 collective-permute-done.2
  392.5 4.6 collective-permute-done.2
  511.5 4.7 collective-permute-done.2
  526.9 5.3 collective-permute-done.2
  543.0 4.4 collective-permute-done.2
  573.0 4.3 collective-permute-done.2
  588.2 4.5 collective-permute-done.2
  603.5 4.1 collective-permute-done.2
  618.5 4.4 collective-permute-done.2
  737.3 4.7 collective-permute-done.2
  752.7 5.3 collective-permute-done.2
  768.8 4.4 collective-permute-done.2
  798.8 4.3 collective-permute-done.2
  814.0 4.5 collective-permute-done.2
  829.3 4.1 collective-permute-done.2
  844.3 4.4 collective-permute-done.2
  963.1 4.7 collective-permute-done.2
  978.5 5.3 collective-permute-done.2
  994.6 4.4 collective-permute-done.2
  1024.6 4.3 collective-permute-done.2
  1039.8 4.5 collective-permute-done.2
  1055.1 4.1 collective-permute-done.2
  1070.1 4.4 collective-permute-done.2
  1129.7 4.0 collective-permute-done.2
  1144.5 4.0 collective-permute-done.2
  1188.8 4.7 collective-permute-done.2
  1204.3 5.3 collective-permute-done.2
  1220.4 4.4 collective-permute-done.2
  1250.4 4.3 collective-permute-done.2
  1265.6 4.5 collective-permute-done.2
  1270.8 129.4 %all_to_all.138 = bf16[8,16,128]{2,1,0:T(8,128)(2,1)S(1)} all-to-all(bf16[8,16,128]{2,1,0:T(8,128)(2,1)S(1)} %bitcast.229), channel_id=1, replica_groups=mesh['ctx'=64,'head'=8] {'head'}, dimensions={0} | all-to-all | bytes 65536 | tf_op jit(solution)/shard_map/all_to_all | solution.py:164
  1400.2 4.0 all-to-all-start.6
  1405.1 6.3 all-to-all-done.6
  1411.4 4.0 all-to-all-start.5
  1416.6 6.8 all-to-all-done.5
  (1147 shorter events, 851.2 us)
Async XLA Ops:
  7.2 272.4 %all-gather.2.cloned.1.call-start = ((), (), s32[]{:S(2)}) async-start(), calls=%async_computation.8 | async-start | bytes 2129920 | tf_op jit(solution)/shard_map/all_gather | solution.py:133
  28.5 12.1 all-to-all-start.2
  40.6 13.7 all-to-all-start.3
  54.3 13.5 all-to-all-start.4
  67.8 238.3 %all-to-all-start.1 = ((bf16[16,8,128]{2,0,1:T(8,128)(2,1)}), bf16[16,8,128]{2,0,1:T(8,128)(2,1)S(1)}, u32[]{:S(2)}, u32[]{:S(2)}) async-start(bf16[16,8,128]{2,0,1:T(8,128)(2,1)} %copy_bitcast_fusion.5), calls=%async_computation.1 | async-start | bytes 65536 | tf_op jit(solution)/shard_map/all_to_all | solution.py:42
  311.5 10.1 collective-permute-start.2
  326.5 9.9 collective-permute-start.2
  341.3 9.9 collective-permute-start.2
  356.1 10.4 collective-permute-start.2
  371.4 10.3 collective-permute-start.2
  386.5 10.5 collective-permute-start.2
  416.7 9.9 collective-permute-start.2
  461.1 9.9 collective-permute-start.2
  505.5 10.6 collective-permute-start.2
  521.0 11.2 collective-permute-start.2
  537.1 10.4 collective-permute-start.2
  567.1 10.3 collective-permute-start.2
  582.2 10.5 collective-permute-start.2
  597.6 10.1 collective-permute-start.2
  612.5 10.3 collective-permute-start.2
  642.5 9.9 collective-permute-start.2
  686.9 9.9 collective-permute-start.2
  731.3 10.6 collective-permute-start.2
  746.8 11.2 collective-permute-start.2
  762.9 10.4 collective-permute-start.2
  778.1 9.9 collective-permute-start.2
  792.9 10.3 collective-permute-start.2
  808.0 10.5 collective-permute-start.2
  823.4 10.1 collective-permute-start.2
  838.3 10.3 collective-permute-start.2
  868.3 9.9 collective-permute-start.2
  912.7 9.9 collective-permute-start.2
  957.1 10.6 collective-permute-start.2
  972.6 11.2 collective-permute-start.2
  988.7 10.4 collective-permute-start.2
  1018.7 10.3 collective-permute-start.2
  1033.8 10.5 collective-permute-start.2
  1049.2 10.1 collective-permute-start.2
  1064.1 10.3 collective-permute-start.2
  1094.1 9.9 collective-permute-start.2
  1138.5 9.9 collective-permute-start.2
  1182.9 10.6 collective-permute-start.2
  1198.4 11.2 collective-permute-start.2
  1214.5 10.4 collective-permute-start.2
  1244.5 10.3 collective-permute-start.2
  1259.6 10.5 collective-permute-start.2
  1400.2 11.2 all-to-all-start.6
  1411.4 12.0 all-to-all-start.5
  (154 other events, 1453.6 us)
Sparse Core Ops, SparseCore 0:
  27.1 252.4 all-gather.1
where the time goes:
time: 1440 us; the launch traced here: 1430 us
  waiting for transfers between devices  750 us (52%)
  starting transfers between devices  394 us (27%)
  blocking collectives  148 us (10%)
  matrix products  83.2 us (6%)
  other arithmetic  16.6 us (1%)
  local copies, waits for them, and re-layouts  15.7 us (1%)
    ppermute x192, waiting for transfers between devices, shifted(): lax.ppermute(array, axis, [(i, (i + by) % size) for i in range(size)])  512 us
    ppermute x192, starting transfers between devices, shifted(): lax.ppermute(array, axis, [(i, (i + by) % size) for i in range(size)])  369 us
    all_gather x1, waiting for transfers between devices, on_device(): portion = lax.all_gather(key_loc, 'ctx', axis=0, tiled=True)  207 us
    all_to_all x1, blocking collectives, on_device(): lax.all_to_all(value_part, 'head', split_axis=0, concat_axis=1, tiled=True)  129 us
    dot_general x80, matrix products, scores_of(): jnp.einsum('rcgd,ncd->rcgn', heads_of_queries, key_split, preferred_eleme...  31.8 us
  transfers between devices with their start and end apart: 199, of which 198 were waited for; matrix products, arithmetic and copies ran while one was open for 8% of the time, Pallas kernels for 0%

commit v1 on v0

v1 whole, which is shorter than its diff:
```python
import functools
import math

import jax
import jax.numpy as jnp
from jax import lax
from jax.experimental import pallas as pl
from jax.experimental.pallas import tpu as pltpu
from jax.sharding import PartitionSpec as P

QUERY_HEADS = 32
KEY_VALUE_HEADS = 8
GROUP = 4
WIDTH = 128
CH = 64
HEADS = 8
NX = 4
NJ = 16
OWN = 16
BLOCK = 128
QT = NX * BLOCK
KT = NJ * BLOCK
KB = 512
SCALE = 1.0 / math.sqrt(WIDTH)
SCALE2 = SCALE * math.log2(math.e)
LOW = -1e30
FLOOR = -1e20

MESH = pl.DeviceIdType.MESH
VMEM = pl.BlockSpec(memory_space=pltpu.VMEM)
SMEM = pl.BlockSpec(memory_space=pltpu.SMEM)
NT = (((1,), (1,)), ((), ()))
TN = (((0,), (0,)), ((), ()))


def place():
    ctx = lax.axis_index("ctx")
    return ctx // NJ, lax.rem(ctx, NJ), lax.axis_index("head")


def head_peer(i, j, h, d):
    return {"ctx": i * NJ + j, "head": lax.rem(h + d, HEADS)}


def x_peer(i, j, h, d):
    return {"ctx": lax.rem(i + d, NX) * NJ + j, "head": h}


def j_peer(i, j, h, d):
    return {"ctx": i * NJ + lax.rem(j + d, NJ), "head": h}


def greet(peers):
    barrier = pltpu.get_barrier_semaphore()
    for peer in peers:
        pl.semaphore_signal(barrier, inc=1, device_id=peer, device_id_type=MESH)
    pl.semaphore_wait(barrier, len(peers))


def remote(src, dst, send, recv, peer):
    return pltpu.make_async_remote_copy(
        src_ref=src, dst_ref=dst, send_sem=send, recv_sem=recv, device_id=peer, device_id_type=MESH
    )


def cols(index, width):
    return pl.ds(pl.multiple_of(index * width, width), width)


def gather_kernel(
    q_ref, g_ref, k_ref, v_ref, e_ref, qa, ga, ka, va, ea,
    local_sem, send1, recv1, send2, recv2, send3, recv3,
):
    i, j, h = place()
    greet(
        [head_peer(i, j, h, d) for d in range(1, HEADS)]
        + [x_peer(i, j, h, d) for d in range(1, NX)]
        + [j_peer(i, j, h, d) for d in range(1, NJ)]
    )

    def pieces(c):
        mine_q = cols(i * HEADS + h, OWN)
        mine_k = cols(j * HEADS + h, OWN)
        mine_e = cols(i * HEADS + h, 8)
        return [
            (k_ref.at[:, cols(c, WIDTH)], ka.at[mine_k, :]),
            (v_ref.at[:, cols(c, WIDTH)], va.at[mine_k, :]),
            (q_ref.at[:, cols(c, GROUP * WIDTH)], qa.at[mine_q, :]),
            (g_ref.at[:, cols(c, GROUP * WIDTH)], ga.at[mine_q, :]),
            (e_ref.at[cols(c, 8), :], ea.at[mine_e, :]),
        ]

    first = []
    for d in range(1, HEADS):
        for n, (src, dst) in enumerate(pieces(lax.rem(h + d, HEADS))):
            copy = remote(src, dst, send1.at[d, n], recv1.at[d, n], head_peer(i, j, h, d))
            copy.start()
            first.append((n, copy))
    own = []
    for n, (src, dst) in enumerate(pieces(h)):
        copy = pltpu.make_async_copy(src, dst, local_sem.at[n])
        copy.start()
        own.append((n, copy))
    for n, copy in own:
        copy.wait()
    for n, copy in first:
        if n < 2:
            copy.wait_recv()
    second = []
    for d in range(1, NJ):
        rows = cols(j, BLOCK)
        for n, ref in enumerate((ka, va)):
            copy = remote(
                ref.at[rows, :], ref.at[rows, :], send3.at[d, n], recv3.at[d, n], j_peer(i, j, h, d)
            )
            copy.start()
            second.append(copy)
    for n, copy in first:
        if n >= 2:
            copy.wait_recv()
    for d in range(1, NX):
        rows = cols(i, BLOCK)
        erows = cols(i, HEADS * 8)
        for n, (ref, part) in enumerate(((qa, rows), (ga, rows), (ea, erows))):
            copy = remote(
                ref.at[part, :], ref.at[part, :], send2.at[d, n], recv2.at[d, n], x_peer(i, j, h, d)
            )
            copy.start()
            second.append(copy)
    for copy in second:
        copy.wait_recv()
    for n, copy in first:
        copy.wait_send()
    for copy in second:
        copy.wait_send()


def gather(queries, grads, keys, values, extra):
    shapes = (
        jax.ShapeDtypeStruct((QT, GROUP * WIDTH), jnp.bfloat16),
        jax.ShapeDtypeStruct((QT, GROUP * WIDTH), jnp.bfloat16),
        jax.ShapeDtypeStruct((KT, WIDTH), jnp.bfloat16),
        jax.ShapeDtypeStruct((KT, WIDTH), jnp.bfloat16),
        jax.ShapeDtypeStruct((NX * HEADS * 8, 128), jnp.float32),
    )
    dma = pltpu.SemaphoreType.DMA
    return pl.pallas_call(
        gather_kernel,
        out_shape=shapes,
        in_specs=[VMEM] * 5,
        out_specs=[VMEM] * 5,
        scratch_shapes=[
            dma((5,)),
            dma((HEADS, 5)),
            dma((HEADS, 5)),
            dma((NX, 3)),
            dma((NX, 3)),
            dma((NJ, 2)),
            dma((NJ, 2)),
        ],
        compiler_params=pltpu.CompilerParams(collective_id=0, has_side_effects=True),
        name="gather",
    )(queries, grads, keys, values, extra)


def masked_scores(spans, start, qpos, key_block, query_head):
    scores = lax.dot_general(key_block, query_head, NT, preferred_element_type=jnp.float32)
    row = lax.broadcasted_iota(jnp.int32, (CH, QT), 0) - qpos
    count = key_block.shape[0] // CH
    parts = [
        jnp.where(row <= -CH * spans[start + n], scores[n * CH : (n + 1) * CH], LOW)
        for n in range(count)
    ]
    return jnp.concatenate(parts, axis=0)


def stats_kernel(spans, qpos_ref, q_ref, k_ref, out_ref):
    qpos = qpos_ref[...]

    def step(b, carry):
        key_block = k_ref[pl.ds(pl.multiple_of(b * KB, KB), KB), :]
        following = []
        for g in range(GROUP):
            top, total = carry[g]
            scores = masked_scores(
                spans, b * (KB // CH), qpos, key_block, q_ref[:, g * WIDTH : (g + 1) * WIDTH]
            )
            new_top = jnp.maximum(top, jnp.max(scores, axis=0, keepdims=True))
            total = total * jnp.exp2((top - new_top) * SCALE2) + jnp.sum(
                jnp.exp2((scores - new_top) * SCALE2), axis=0, keepdims=True
            )
            following.append((new_top, total))
        return tuple(following)

    start = tuple(
        (jnp.full((1, QT), FLOOR, jnp.float32), jnp.zeros((1, QT), jnp.float32))
        for g in range(GROUP)
    )
    result = lax.fori_loop(0, KT // KB, step, start)
    for g in range(GROUP):
        out_ref[g : g + 1, :] = result[g][0]
        out_ref[GROUP + g : GROUP + g + 1, :] = result[g][1]


def stats(spans, qpos, queries, keys):
    return pl.pallas_call(
        stats_kernel,
        out_shape=jax.ShapeDtypeStruct((2 * GROUP, QT), jnp.float32),
        in_specs=[SMEM, VMEM, VMEM, VMEM],
        out_specs=VMEM,
        name="stats",
    )(spans, qpos, queries, keys)


def share_kernel(in_ref, out_ref, local_sem, send, recv):
    i, j, h = place()
    greet([x_peer(i, j, h, d) for d in range(1, NX)])
    mine = out_ref.at[cols(i, 2 * GROUP), :]
    copies = []
    for d in range(1, NX):
        copy = remote(in_ref, mine, send.at[d], recv.at[d], x_peer(i, j, h, d))
        copy.start()
        copies.append(copy)
    own = pltpu.make_async_copy(in_ref, mine, local_sem)
    own.start()
    own.wait()
    for copy in copies:
        copy.wait_recv()
    for copy in copies:
        copy.wait_send()


def share(values):
    dma = pltpu.SemaphoreType.DMA
    return pl.pallas_call(
        share_kernel,
        out_shape=jax.ShapeDtypeStruct((NX * 2 * GROUP, QT), jnp.float32),
        in_specs=[VMEM],
        out_specs=VMEM,
        scratch_shapes=[dma, dma((NX,)), dma((NX,))],
        compiler_params=pltpu.CompilerParams(collective_id=1, has_side_effects=True),
        name="share",
    )(values)


def grads_kernel(
    spans, qpos_ref, stats_ref, extra_ref, q_ref, g_ref, k_ref, v_ref, dq_ref, dk_ref, dv_ref, acc
):
    qpos = qpos_ref[...]
    gain = extra_ref[GROUP : GROUP + 1, :]
    gain_scale = gain * SCALE
    norms = []
    for g in range(GROUP):
        tops = [stats_ref[x * 2 * GROUP + g :][:1, :] for x in range(NX)]
        totals = [stats_ref[x * 2 * GROUP + GROUP + g :][:1, :] for x in range(NX)]
        top = functools.reduce(jnp.maximum, tops)
        total = sum(t * jnp.exp2((m - top) * SCALE2) for m, t in zip(tops, totals))
        norms.append(top * SCALE2 + jnp.log2(total))
    acc[...] = jnp.zeros_like(acc)

    def step(b, carry):
        rows = pl.ds(pl.multiple_of(b * KB, KB), KB)
        key_block = k_ref[rows, :]
        value_block = v_ref[rows, :]
        key_grad = jnp.zeros((KB, WIDTH), jnp.float32)
        value_grad = jnp.zeros((KB, WIDTH), jnp.float32)
        for g in range(GROUP):
            part = slice(g * WIDTH, (g + 1) * WIDTH)
            query_head = q_ref[:, part]
            grad_head = g_ref[:, part]
            scores = masked_scores(spans, b * (KB // CH), qpos, key_block, query_head)
            probs = jnp.exp2(scores * SCALE2 - norms[g])
            prob_grads = lax.dot_general(
                value_block, grad_head, NT, preferred_element_type=jnp.float32
            )
            out_dot = extra_ref[g : g + 1, :]
            weighted = (probs * gain).astype(jnp.bfloat16)
            score_grads = (probs * ((prob_grads - out_dot) * gain_scale)).astype(jnp.bfloat16)
            key_grad += jnp.dot(score_grads, query_head, preferred_element_type=jnp.float32)
            value_grad += jnp.dot(weighted, grad_head, preferred_element_type=jnp.float32)
            acc[:, part] += lax.dot_general(
                score_grads, key_block, TN, preferred_element_type=jnp.float32
            )
        dk_ref[rows, :] = key_grad.astype(jnp.bfloat16)
        dv_ref[rows, :] = value_grad.astype(jnp.bfloat16)
        return carry

    lax.fori_loop(0, KT // KB, step, 0)
    dq_ref[...] = acc[...].astype(jnp.bfloat16)


def grads(spans, qpos, all_stats, extra, queries, out_grads, keys, values):
    return pl.pallas_call(
        grads_kernel,
        out_shape=(
            jax.ShapeDtypeStruct((QT, GROUP * WIDTH), jnp.bfloat16),
            jax.ShapeDtypeStruct((KT, WIDTH), jnp.bfloat16),
            jax.ShapeDtypeStruct((KT, WIDTH), jnp.bfloat16),
        ),
        in_specs=[SMEM] + [VMEM] * 7,
        out_specs=[VMEM] * 3,
        scratch_shapes=[pltpu.VMEM((QT, GROUP * WIDTH), jnp.float32)],
        name="grads",
    )(spans, qpos, all_stats, extra, queries, out_grads, keys, values)


def scatter_kernel(
    dq_ref, dk_ref, dv_ref, oq, ok, ov, rq, rk, rv, sq, sk, sv,
    local_sem, send1, recv1, send2, recv2, send3, recv3,
):
    i, j, h = place()
    greet(
        [head_peer(i, j, h, d) for d in range(1, HEADS)]
        + [x_peer(i, j, h, d) for d in range(1, NX)]
        + [j_peer(i, j, h, d) for d in range(1, NJ)]
    )
    pairs = []
    for d in range(1, NJ):
        rows = cols(lax.rem(j + d, NJ), BLOCK)
        for n, (src, dst) in enumerate(((dk_ref, rk), (dv_ref, rv))):
            copy = remote(
                src.at[rows, :], dst.at[d - 1], send3.at[d, n], recv3.at[d, n], j_peer(i, j, h, d)
            )
            copy.start()
            pairs.append(copy)
    query_parts = []
    for d in range(1, NX):
        rows = cols(lax.rem(i + d, NX), BLOCK)
        copy = remote(dq_ref.at[rows, :], rq.at[d - 1], send1.at[d], recv1.at[d], x_peer(i, j, h, d))
        copy.start()
        query_parts.append(copy)
    for copy in query_parts:
        copy.wait_recv()
    total = dq_ref[cols(i, BLOCK), :].astype(jnp.float32)
    for d in range(1, NX):
        total += rq[d - 1].astype(jnp.float32)
    sq[...] = total.astype(jnp.bfloat16)
    for copy in pairs:
        copy.wait_recv()
    for src, dst, out in ((dk_ref, rk, sk), (dv_ref, rv, sv)):
        total = src[cols(j, BLOCK), :].astype(jnp.float32)
        for d in range(1, NJ):
            total += dst[d - 1].astype(jnp.float32)
        out[...] = total.astype(jnp.bfloat16)

    def pieces(c):
        rows = cols(c, OWN)
        return [
            (sq.at[rows, :], oq.at[:, cols(h, GROUP * WIDTH)]),
            (sk.at[rows, :], ok.at[:, cols(h, WIDTH)]),
            (sv.at[rows, :], ov.at[:, cols(h, WIDTH)]),
        ]

    last = []
    for d in range(1, HEADS):
        for n, (src, dst) in enumerate(pieces(lax.rem(h + d, HEADS))):
            copy = remote(src, dst, send2.at[d, n], recv2.at[d, n], head_peer(i, j, h, d))
            copy.start()
            last.append(copy)
    own = []
    for n, (src, dst) in enumerate(pieces(h)):
        copy = pltpu.make_async_copy(src, dst, local_sem.at[n])
        copy.start()
        own.append(copy)
    for copy in own:
        copy.wait()
    for copy in last:
        copy.wait_recv()
    for copy in pairs + query_parts + last:
        copy.wait_send()


def scatter(dq, dk, dv):
    dma = pltpu.SemaphoreType.DMA
    bf16 = jnp.bfloat16
    return pl.pallas_call(
        scatter_kernel,
        out_shape=(
            jax.ShapeDtypeStruct((OWN, QUERY_HEADS * WIDTH), bf16),
            jax.ShapeDtypeStruct((OWN, KEY_VALUE_HEADS * WIDTH), bf16),
            jax.ShapeDtypeStruct((OWN, KEY_VALUE_HEADS * WIDTH), bf16),
        ),
        in_specs=[VMEM] * 3,
        out_specs=[VMEM] * 3,
        scratch_shapes=[
            pltpu.VMEM((NX - 1, BLOCK, GROUP * WIDTH), bf16),
            pltpu.VMEM((NJ - 1, BLOCK, WIDTH), bf16),
            pltpu.VMEM((NJ - 1, BLOCK, WIDTH), bf16),
            pltpu.VMEM((BLOCK, GROUP * WIDTH), bf16),
            pltpu.VMEM((BLOCK, WIDTH), bf16),
            pltpu.VMEM((BLOCK, WIDTH), bf16),
            dma((3,)),
            dma((NX,)),
            dma((NX,)),
            dma((HEADS, 3)),
            dma((HEADS, 3)),
            dma((NJ, 2)),
            dma((NJ, 2)),
        ],
        compiler_params=pltpu.CompilerParams(collective_id=2, has_side_effects=True),
        name="scatter",
    )(dq, dk, dv)


def on_device(queries, keys, values, outputs, output_gradient, importance, span_order):
    i, j, h = place()
    out_dot = jnp.sum(
        (output_gradient.astype(jnp.float32) * outputs.astype(jnp.float32)).reshape(
            OWN, KEY_VALUE_HEADS, GROUP, WIDTH
        ),
        axis=-1,
    ).transpose(1, 2, 0)
    own_gain = lax.dynamic_slice_in_dim(importance.astype(jnp.float32) * 0.25, h * OWN, OWN)
    extra = jnp.concatenate(
        [out_dot, jnp.broadcast_to(own_gain, (KEY_VALUE_HEADS, 1, OWN))], axis=1
    )
    extra = jnp.pad(extra, ((0, 0), (0, 8 - GROUP - 1), (0, 128 - OWN)))
    qa, ga, ka, va, ea = gather(
        queries, output_gradient, keys, values, extra.reshape(KEY_VALUE_HEADS * 8, 128)
    )
    extra_all = ea.reshape(NX, HEADS, 8, 128)[..., :OWN].transpose(2, 0, 1, 3).reshape(8, QT)
    query_spans = lax.dynamic_index_in_dim(span_order.reshape(NX, NJ, 2), j, 1, keepdims=False)
    qpos = (query_spans.reshape(-1, 1) * CH + jnp.arange(CH, dtype=jnp.int32)).reshape(1, QT)
    spans = lax.dynamic_slice_in_dim(span_order, i * (KT // CH), KT // CH)
    own_stats = stats(spans, qpos, qa, ka)
    all_stats = share(own_stats)
    dq, dk, dv = grads(spans, qpos, all_stats, extra_all, qa, ga, ka, va)
    return scatter(dq, dk, dv)


def solution(mesh):
    tokens = P(("ctx", "head"), None)
    return jax.shard_map(
        on_device,
        mesh=mesh,
        in_specs=(tokens, tokens, tokens, tokens, tokens, P("ctx"), P()),
        out_specs=(tokens, tokens, tokens),
        check_vma=False,
    )
```

time: 1440 us -> 138 us (0.10)
  waiting for transfers between devices: 750 us -> 0 us
  starting transfers between devices: 394 us -> 0 us
  blocking collectives: 148 us -> 0 us
  Pallas kernels: 0 us -> 127 us
  matrix products: 83.2 us -> 0 us
  other arithmetic: 16.6 us -> 1.32 us
    ppermute x192 -> x0, waiting for transfers between devices: 512 us -> none  [shifted(): lax.ppermute(array, axis, [(i, (i + by) % size) for i in range(size)])]
    ppermute x192 -> x0, starting transfers between devices: 369 us -> none  [shifted(): lax.ppermute(array, axis, [(i, (i + by) % size) for i in range(size)])]
    all_gather x1 -> x0, waiting for transfers between devices: 207 us -> none  [on_device(): portion = lax.all_gather(key_loc, 'ctx', axis=0, tiled=True)]
    all_to_all x2 -> x0, blocking collectives: 148 us -> none  [the longest x1 129 us: on_device(): lax.all_to_all(value_part, 'head', split_axis=0, concat_axis=1, tiled=True)]
    pallas_call x0 -> x5, Pallas kernels: none -> 127 us  [the longest x1 50.9 us: gather(): pl.pallas_call(gather_kernel, out_shape=shapes, in_specs=[VMEM] * 5, out_...]
    dot_general x336 -> x0, matrix products: 83.2 us -> none  [the longest x80 31.8 us: scores_of(): jnp.einsum('rcgd,ncd->rcgn', heads_of_queries, key_split, preferred_eleme...]
    all_to_all x6 -> x0, waiting for transfers between devices: 31 us -> none  [the longest x1 7.53 us: on_device(): lax.all_to_all(outputs, 'head', split_axis=1, concat_axis=0, tiled=True)]
    all_to_all x6 -> x0, starting transfers between devices: 25.5 us -> none  [the longest x1 4.97 us: on_device(): lax.all_to_all(output_gradient, 'head', split_axis=1, concat_axis=0, tile...]
  transfers between devices with their start and end apart: 199 -> 0, of which waited for: 198 -> 0; matrix products, arithmetic and copies ran while one was open for 8% -> 0% of each run, Pallas kernels for 0% -> 0%
where the time goes in v1:
time: 138 us; the launch traced here: 137 us
  Pallas kernels  127 us (92%)
  local copies, waits for them, and re-layouts  7.8 us (6%)
    pallas_call x1, Pallas kernels, gather(): pl.pallas_call(gather_kernel, out_shape=shapes, in_specs=[VMEM] * 5, out_...  50.9 us
    pallas_call x1, Pallas kernels, scatter(): pl.pallas_call(scatter_kernel, out_shape=(jax.ShapeDtypeStruct((OWN, QUER...  45.7 us
    pallas_call x1, Pallas kernels, grads(): pl.pallas_call(grads_kernel, out_shape=(jax.ShapeDtypeStruct((QT, GROUP *...  16.2 us
    pallas_call x1, Pallas kernels, stats(): pl.pallas_call(stats_kernel, out_shape=jax.ShapeDtypeStruct((2 * GROUP, Q...  7.42 us
    pallas_call x1, Pallas kernels, share(): pl.pallas_call(share_kernel, out_shape=jax.ShapeDtypeStruct((NX * 2 * GRO...  7.02 us
    unnamed x13, local copies, waits for them, and re-layouts  4.66 us

profile of v1, /device:TPU:1, one launch (start us, length us, event | category | flops | bytes accessed | tf_op | source)
XLA Modules:
  0.0 137.1 jit_solution(137865503914836165)
XLA Ops:
  0.7 0.0 copy-start.2
  0.7 0.6 copy-done.2
  1.3 0.0 copy-start.3
  1.3 0.5 dynamic_slice.10.spans
  1.9 0.1 copy-done.3
  2.0 0.1 dynamic_slice.12
  2.1 0.1 reshape.55
  2.2 0.1 mul.28
  2.3 0.1 iota_add_fusion
  2.4 0.7 add.41.qpos_ref
  3.0 1.0 convert_multiply_fusion
  4.0 0.2 reshape.56
  4.2 0.2 reduce_sum.9
  4.4 0.1 copy.14
  4.6 0.6 pad_bitcast_fusion.e_ref
  5.2 50.9 %gather.1 = (bf16[512,512]{1,0:T(8,128)(2,1)}, bf16[512,512]{1,0:T(8,128)(2,1)}, bf16[2048,128]{1,0:T(8,128)(2,1)}, bf16[2048,128]{1,0:T(8,128)(2,1)}, f32[256,128]{1,0:T(8,128)}) custom-call(bf16[16,4096]{1,0:T(8,128)(2,1)} %q_ref.1, bf16[16,4096]{1,0:T(8,128)(2,1)} %g_ref.1, bf16[16,1024]{1,0:T(8,128)(2,1)} %k_ref.1, bf16[16,1024]{1,0:T(8,128)(2,1)} %v_ref.1, ...), custom_call_target="tpu_custom_call" | custom-call | tf_op jit(solution)/shard_map/gather/pallas_call | solution.py:147
  56.1 0.9 copy.20
  57.1 0.7 reshape.59.extra_ref
  57.8 7.4 %stats.1.in_ref = f32[8,512]{1,0:T(8,128)} custom-call(s32[32]{0:T(128)} %dynamic_slice.10.spans, s32[1,512]{1,0:T(1,128)} %add.41.qpos_ref, bf16[512,512]{1,0:T(8,128)(2,1)} %get-tuple-element.11.q_ref, bf16[2048,128]{1,0:T(8,128)(2,1)} %get-tuple-element.12.k_ref), custom_call_target="tpu_custom_call" | custom-call | tf_op jit(solution)/shard_map/stats/pallas_call | solution.py:206
  65.2 7.0 %share.1.stats_ref = f32[32,512]{1,0:T(8,128)} custom-call(f32[8,512]{1,0:T(8,128)} %stats.1.in_ref), custom_call_target="tpu_custom_call" | custom-call | tf_op jit(solution)/shard_map/share/pallas_call | solution.py:235
  72.2 16.2 %grads.1 = (bf16[512,512]{1,0:T(8,128)(2,1)}, bf16[2048,128]{1,0:T(8,128)(2,1)}, bf16[2048,128]{1,0:T(8,128)(2,1)}) custom-call(s32[32]{0:T(128)} %dynamic_slice.10.spans, s32[1,512]{1,0:T(1,128)} %add.41.qpos_ref, f32[32,512]{1,0:T(8,128)} %share.1.stats_ref, f32[8,512]{1,0:T(8,128)} %reshape.59.extra_ref, bf16[512,512]{1,0:T(8,128)(2,1)} %get-tuple-element.11.q_ref, ...), custom_call_target="tpu_custom_call" | custom-call | tf_op jit(solution)/shard_map/grads/pallas_call | solution.py:293
  88.4 45.7 %scatter.1 = (bf16[16,4096]{1,0:T(8,128)(2,1)}, bf16[16,1024]{1,0:T(8,128)(2,1)}, bf16[16,1024]{1,0:T(8,128)(2,1)}) custom-call(bf16[512,512]{1,0:T(8,128)(2,1)} %get-tuple-element.16.dq_ref, bf16[2048,128]{1,0:T(8,128)(2,1)} %get-tuple-element.17.dk_ref, bf16[2048,128]{1,0:T(8,128)(2,1)} %get-tuple-element.18.dv_ref), custom_call_target="tpu_custom_call" | custom-call | tf_op jit(solution)/shard_map/scatter/pallas_call | solution.py:376
  134.1 0.0 copy-start.1
  134.1 1.6 %copy.24 = bf16[16,4096]{1,0:T(8,128)(2,1)} copy(bf16[16,4096]{1,0:T(8,128)(2,1)} %get-tuple-element.22) | data formatting | bytes 262144
  135.7 0.0 copy-done.1
  135.7 0.0 copy-start
  135.7 0.6 copy.25
  136.3 0.2 copy-done
  136.4 0.6 copy.26
  (5 shorter events, 0.1 us)
Async XLA Ops:
  0.7 0.7 copy-start.2
  1.3 0.7 copy-start.3
  134.1 1.6 %copy-start.1 = (bf16[16,1024]{1,0:T(8,128)(2,1)S(1)}, bf16[16,1024]{1,0:T(8,128)(2,1)}, u32[]{:S(2)}) copy-start(bf16[16,1024]{1,0:T(8,128)(2,1)} %get-tuple-element.23) | copy-start | bytes 98308
  135.7 0.8 copy-start

commit v2 on v1

--- a/solution.py
+++ b/solution.py
@@ -16,6 +16,7 @@
 HEADS = 8
 NX = 4
 NJ = 16
+NY = 8
 OWN = 16
 BLOCK = 128
 QT = NX * BLOCK
@@ -46,10 +47,6 @@
     return {"ctx": lax.rem(i + d, NX) * NJ + j, "head": h}
 
 
-def j_peer(i, j, h, d):
-    return {"ctx": i * NJ + lax.rem(j + d, NJ), "head": h}
-
-
 def greet(peers):
     barrier = pltpu.get_barrier_semaphore()
     for peer in peers:
@@ -67,32 +64,49 @@
     return pl.ds(pl.multiple_of(index * width, width), width)
 
 
+def z_peer(i, j, h):
+    return {"ctx": i * NJ + lax.rem(j + NY, NJ), "head": h}
+
+
+def y_peer(i, j, h, d):
+    return {"ctx": i * NJ + (j // NY) * NY + lax.rem(lax.rem(j, NY) + d + NY, NY), "head": h}
+
+
+def ring_block(j, zc, d):
+    other = lax.rem(j // NY + zc, 2)
+    return other * NY + lax.rem(lax.rem(j, NY) + d + 2 * NY, NY)
+
+
+def all_peers(i, j, h):
+    return (
+        [head_peer(i, j, h, d) for d in range(1, HEADS)]
+        + [x_peer(i, j, h, d) for d in range(1, NX)]
+        + [z_peer(i, j, h), y_peer(i, j, h, 1), y_peer(i, j, h, -1)]
+    )
+
+
 def gather_kernel(
-    q_ref, g_ref, k_ref, v_ref, e_ref, qa, ga, ka, va, ea,
-    local_sem, send1, recv1, send2, recv2, send3, recv3,
+    q_ref, g_ref, k_ref, v_ref, e_ref, qa, ga, ka, va, ea, ep,
+    local_sem, send1, recv1, send2, recv2, send3, recv3, send4, recv4, send5, recv5,
 ):
     i, j, h = place()
-    greet(
-        [head_peer(i, j, h, d) for d in range(1, HEADS)]
-        + [x_peer(i, j, h, d) for d in range(1, NX)]
-        + [j_peer(i, j, h, d) for d in range(1, NJ)]
-    )
+    greet(all_peers(i, j, h))
 
     def pieces(c):
         mine_q = cols(i * HEADS + h, OWN)
         mine_k = cols(j * HEADS + h, OWN)
-        mine_e = cols(i * HEADS + h, 8)
         return [
             (k_ref.at[:, cols(c, WIDTH)], ka.at[mine_k, :]),
             (v_ref.at[:, cols(c, WIDTH)], va.at[mine_k, :]),
             (q_ref.at[:, cols(c, GROUP * WIDTH)], qa.at[mine_q, :]),
             (g_ref.at[:, cols(c, GROUP * WIDTH)], ga.at[mine_q, :]),
-            (e_ref.at[cols(c, 8), :], ea.at[mine_e, :]),
+            (e_ref.at[cols(c, 8), :], ep.at[cols(h, 8), :]),
         ]
 
     first = []
-    for d in range(1, HEADS):
-        for n, (src, dst) in enumerate(pieces(lax.rem(h + d, HEADS))):
+    for n in range(5):
+        for d in range(1, HEADS):
+            src, dst = pieces(lax.rem(h + d, HEADS))[n]
             copy = remote(src, dst, send1.at[d, n], recv1.at[d, n], head_peer(i, j, h, d))
             copy.start()
             first.append((n, copy))
@@ -100,38 +114,82 @@
     for n, (src, dst) in enumerate(pieces(h)):
         copy = pltpu.make_async_copy(src, dst, local_sem.at[n])
         copy.start()
-        own.append((n, copy))
-    for n, copy in own:
+        own.append(copy)
+    for copy in own:
         copy.wait()
     for n, copy in first:
         if n < 2:
             copy.wait_recv()
-    second = []
-    for d in range(1, NJ):
-        rows = cols(j, BLOCK)
-        for n, ref in enumerate((ka, va)):
-            copy = remote(
-                ref.at[rows, :], ref.at[rows, :], send3.at[d, n], recv3.at[d, n], j_peer(i, j, h, d)
+    sent = []
+
+    def push(ref, rows, send, recv, peer):
+        copy = remote(ref.at[rows, :], ref.at[rows, :], send, recv, peer)
+        copy.start()
+        sent.append(copy)
+        return copy
+
+    pair = (ka, va)
+    ways = (1, -1)
+    ring = {}
+
+    def ring_push(step, zc, way, kinds):
+        rows = cols(ring_block(j, zc, -ways[way] * (step - 1)), BLOCK)
+        for n in kinds:
+            at = (way, step - 1, zc, n)
+            ring[way, step, zc, n] = push(
+                pair[n], rows, send3.at[at], recv3.at[at], y_peer(i, j, h, ways[way])
             )
-            copy.start()
-            second.append(copy)
+
+    across = [
+        push(pair[n], cols(j, BLOCK), send4.at[n], recv4.at[n], z_peer(i, j, h)) for n in range(2)
+    ]
+    for way in range(2):
+        ring_push(1, 0, way, (0, 1))
     for n, copy in first:
         if n >= 2:
             copy.wait_recv()
-    for d in range(1, NX):
-        rows = cols(i, BLOCK)
-        erows = cols(i, HEADS * 8)
-        for n, (ref, part) in enumerate(((qa, rows), (ga, rows), (ea, erows))):
-            copy = remote(
-                ref.at[part, :], ref.at[part, :], send2.at[d, n], recv2.at[d, n], x_peer(i, j, h, d)
-            )
-            copy.start()
-            second.append(copy)
-    for copy in second:
+    x_rows = cols(i, BLOCK)
+    x_first = [
+        [
+            push(ref, x_rows, send2.at[way, 0, n], recv2.at[way, 0, n], x_peer(i, j, h, d))
+            for n, ref in enumerate((qa, ga))
+        ]
+        for way, d in enumerate((1, NX - 1))
+    ]
+    for copy in across:
+        copy.wait_recv()
+    for way in range(2):
+        ring_push(1, 1, way, (0, 1))
+    ea[cols(i, 8), :] = jnp.concatenate(
+        [ep[8 * n : 8 * n + 8, :OWN] for n in range(HEADS)], axis=1
+    )
+    extras = [
+        push(ea, cols(i, 8), send5.at[d], recv5.at[d], x_peer(i, j, h, d)) for d in range(1, NX)
+    ]
+    for step in range(2, 5):
+        for zc in range(2):
+            for way in range(2):
+                for n in range(2):
+                    ring[way, step - 1, zc, n].wait_recv()
+                ring_push(step, zc, way, (0, 1) if step < 4 else (way,))
+        if step == 3:
+            for copies in x_first:
+                for copy in copies:
+                    copy.wait_recv()
+            x_last = []
+            for way, (ref, d) in enumerate(((qa, 1), (ga, NX - 1))):
+                rows = cols(lax.rem(i - (1, -1)[way] + NX, NX), BLOCK)
+                x_last.append(
+                    push(ref, rows, send2.at[way, 1, 0], recv2.at[way, 1, 0], x_peer(i, j, h, d))
+                )
+    for zc in range(2):
+        for way in range(2):
+            ring[way, 4, zc, way].wait_recv()
+    for copy in x_last + extras:
         copy.wait_recv()
     for n, copy in first:
         copy.wait_send()
-    for copy in second:
+    for copy in sent:
         copy.wait_send()
 
 
@@ -141,7 +199,7 @@
         jax.ShapeDtypeStruct((QT, GROUP * WIDTH), jnp.bfloat16),
         jax.ShapeDtypeStruct((KT, WIDTH), jnp.bfloat16),
         jax.ShapeDtypeStruct((KT, WIDTH), jnp.bfloat16),
-        jax.ShapeDtypeStruct((NX * HEADS * 8, 128), jnp.float32),
+        jax.ShapeDtypeStruct((NX * 8, 128), jnp.float32),
     )
     dma = pltpu.SemaphoreType.DMA
     return pl.pallas_call(
@@ -150,17 +208,37 @@
         in_specs=[VMEM] * 5,
         out_specs=[VMEM] * 5,
         scratch_shapes=[
+            pltpu.VMEM((HEADS * 8, 128), jnp.float32),
             dma((5,)),
             dma((HEADS, 5)),
             dma((HEADS, 5)),
-            dma((NX, 3)),
-            dma((NX, 3)),
-            dma((NJ, 2)),
-            dma((NJ, 2)),
+            dma((2, 2, 2)),
+            dma((2, 2, 2)),
+            dma((2, 4, 2, 2)),
+            dma((2, 4, 2, 2)),
+            dma((2,)),
+            dma((2,)),
+            dma((NX,)),
+            dma((NX,)),
         ],
         compiler_params=pltpu.CompilerParams(collective_id=0, has_side_effects=True),
         name="gather",
     )(queries, grads, keys, values, extra)
+
+
+def query_positions(spans):
+    i, j, h = place()
+    lane = lax.broadcasted_iota(jnp.int32, (1, BLOCK), 1)
+    rows = []
+    for x in range(NX):
+        at = 2 * (x * NJ + j)
+        start = jnp.where(lane < CH, spans[at] * CH, spans[at + 1] * CH - CH)
+        rows.append(start + lane)
+    return jnp.concatenate(rows, axis=1)
+
+
+def extra_row(extra_ref, n):
+    return jnp.concatenate([extra_ref[8 * x + n : 8 * x + n + 1, :] for x in range(NX)], axis=1)
 
 
 def masked_scores(spans, start, qpos, key_block, query_head):
@@ -174,8 +252,9 @@
     return jnp.concatenate(parts, axis=0)
 
 
-def stats_kernel(spans, qpos_ref, q_ref, k_ref, out_ref):
-    qpos = qpos_ref[...]
+def stats_kernel(spans, q_ref, k_ref, out_ref):
+    qpos = query_positions(spans)
+    first_span = (lax.axis_index("ctx") // NJ) * (KT // CH)
 
     def step(b, carry):
         key_block = k_ref[pl.ds(pl.multiple_of(b * KB, KB), KB), :]
@@ -183,7 +262,7 @@
         for g in range(GROUP):
             top, total = carry[g]
             scores = masked_scores(
-                spans, b * (KB // CH), qpos, key_block, q_ref[:, g * WIDTH : (g + 1) * WIDTH]
+                spans, first_span + b * (KB // CH), qpos, key_block, q_ref[:, g * WIDTH : (g + 1) * WIDTH]
             )
             new_top = jnp.maximum(top, jnp.max(scores, axis=0, keepdims=True))
             total = total * jnp.exp2((top - new_top) * SCALE2) + jnp.sum(
@@ -202,14 +281,14 @@
         out_ref[GROUP + g : GROUP + g + 1, :] = result[g][1]
 
 
-def stats(spans, qpos, queries, keys):
+def stats(spans, queries, keys):
     return pl.pallas_call(
         stats_kernel,
         out_shape=jax.ShapeDtypeStruct((2 * GROUP, QT), jnp.float32),
-        in_specs=[SMEM, VMEM, VMEM, VMEM],
+        in_specs=[SMEM, VMEM, VMEM],
         out_specs=VMEM,
         name="stats",
-    )(spans, qpos, queries, keys)
+    )(spans, queries, keys)
 
 
 def share_kernel(in_ref, out_ref, local_sem, send, recv):
@@ -244,10 +323,12 @@
 
 
 def grads_kernel(
-    spans, qpos_ref, stats_ref, extra_ref, q_ref, g_ref, k_ref, v_ref, dq_ref, dk_ref, dv_ref, acc
+    spans, stats_ref, extra_ref, q_ref, g_ref, k_ref, v_ref, dq_ref, dk_ref, dv_ref, acc
 ):
-    qpos = qpos_ref[...]
-    gain = extra_ref[GROUP : GROUP + 1, :]
+    qpos = query_positions(spans)
+    first_span = (lax.axis_index("ctx") // NJ) * (KT // CH)
+    gain = extra_row(extra_ref, GROUP)
+    out_dots = [extra_row(extra_ref, g) for g in range(GROUP)]
     gain_scale = gain * SCALE
     norms = []
     for g in range(GROUP):
@@ -268,12 +349,12 @@
             part = slice(g * WIDTH, (g + 1) * WIDTH)
             query_head = q_ref[:, part]
             grad_head = g_ref[:, part]
-            scores = masked_scores(spans, b * (KB // CH), qpos, key_block, query_head)
+            scores = masked_scores(spans, first_span + b * (KB // CH), qpos, key_block, query_head)
             probs = jnp.exp2(scores * SCALE2 - norms[g])
             prob_grads = lax.dot_general(
                 value_block, grad_head, NT, preferred_element_type=jnp.float32
             )
-            out_dot = extra_ref[g : g + 1, :]
+            out_dot = out_dots[g]
             weighted = (probs * gain).astype(jnp.bfloat16)
             score_grads = (probs * ((prob_grads - out_dot) * gain_scale)).astype(jnp.bfloat16)
             key_grad += jnp.dot(score_grads, query_head, preferred_element_type=jnp.float32)
@@ -289,7 +370,7 @@
     dq_ref[...] = acc[...].astype(jnp.bfloat16)
 
 
-def grads(spans, qpos, all_stats, extra, queries, out_grads, keys, values):
+def grads(spans, all_stats, extra, queries, out_grads, keys, values):
     return pl.pallas_call(
         grads_kernel,
         out_shape=(
@@ -297,51 +378,87 @@
             jax.ShapeDtypeStruct((KT, WIDTH), jnp.bfloat16),
             jax.ShapeDtypeStruct((KT, WIDTH), jnp.bfloat16),
         ),
-        in_specs=[SMEM] + [VMEM] * 7,
+        in_specs=[SMEM] + [VMEM] * 6,
         out_specs=[VMEM] * 3,
         scratch_shapes=[pltpu.VMEM((QT, GROUP * WIDTH), jnp.float32)],
         name="grads",
-    )(spans, qpos, all_stats, extra, queries, out_grads, keys, values)
+    )(spans, all_stats, extra, queries, out_grads, keys, values)
 
 
 def scatter_kernel(
-    dq_ref, dk_ref, dv_ref, oq, ok, ov, rq, rk, rv, sq, sk, sv,
-    local_sem, send1, recv1, send2, recv2, send3, recv3,
+    dq_ref, dk_ref, dv_ref, oq, ok, ov, rq, rr, run, zs, zr, sq, sk, sv,
+    local_sem, send1, recv1, send2, recv2, send3, recv3, send4, recv4,
 ):
     i, j, h = place()
-    greet(
-        [head_peer(i, j, h, d) for d in range(1, HEADS)]
-        + [x_peer(i, j, h, d) for d in range(1, NX)]
-        + [j_peer(i, j, h, d) for d in range(1, NJ)]
-    )
-    pairs = []
-    for d in range(1, NJ):
-        rows = cols(lax.rem(j + d, NJ), BLOCK)
-        for n, (src, dst) in enumerate(((dk_ref, rk), (dv_ref, rv))):
-            copy = remote(
-                src.at[rows, :], dst.at[d - 1], send3.at[d, n], recv3.at[d, n], j_peer(i, j, h, d)
-            )
-            copy.start()
-            pairs.append(copy)
+    greet(all_peers(i, j, h))
+    sent = []
+
+    def push(src, dst, send, recv, peer):
+        copy = remote(src, dst, send, recv, peer)
+        copy.start()
+        sent.append(copy)
+        return copy
+
+    pair = (dk_ref, dv_ref)
+    ways = (1, -1)
+    ring = {}
+
+    def ring_push(src, way, step, zc, n):
+        at = (way, step - 1, zc, n)
+        ring[way, step, zc, n] = push(
+            src, rr.at[at], send3.at[at], recv3.at[at], y_peer(i, j, h, ways[way])
+        )
+
+    def target(way, step, zc):
+        return cols(ring_block(j, zc, ways[way] * (5 - step)), BLOCK)
+
+    for zc in (1, 0):
+        for way in range(2):
+            ring_push(pair[way].at[target(way, 1, zc), :], way, 1, zc, way)
     query_parts = []
     for d in range(1, NX):
         rows = cols(lax.rem(i + d, NX), BLOCK)
-        copy = remote(dq_ref.at[rows, :], rq.at[d - 1], send1.at[d], recv1.at[d], x_peer(i, j, h, d))
-        copy.start()
-        query_parts.append(copy)
+        query_parts.append(
+            push(dq_ref.at[rows, :], rq.at[d - 1], send1.at[d], recv1.at[d], x_peer(i, j, h, d))
+        )
+    for zc in (1, 0):
+        for way in range(2):
+            ring_push(pair[1 - way].at[target(way, 2, zc), :], way, 2, zc, 1 - way)
+    for step in range(2, 5):
+        for zc in (1, 0):
+            for way in range(2):
+                for n in range(2) if step > 2 else (way,):
+                    ring[way, step - 1, zc, n].wait_recv()
+                    total = rr[way, step - 2, zc, n].astype(jnp.float32) + pair[n][
+                        target(way, step, zc), :
+                    ].astype(jnp.float32)
+                    run[way, step - 2, zc, n] = total.astype(jnp.bfloat16)
+                    ring_push(run.at[way, step - 2, zc, n], way, step, zc, n)
     for copy in query_parts:
         copy.wait_recv()
     total = dq_ref[cols(i, BLOCK), :].astype(jnp.float32)
     for d in range(1, NX):
         total += rq[d - 1].astype(jnp.float32)
     sq[...] = total.astype(jnp.bfloat16)
-    for copy in pairs:
-        copy.wait_recv()
-    for src, dst, out in ((dk_ref, rk, sk), (dv_ref, rv, sv)):
-        total = src[cols(j, BLOCK), :].astype(jnp.float32)
-        for d in range(1, NJ):
-            total += dst[d - 1].astype(jnp.float32)
-        out[...] = total.astype(jnp.bfloat16)
+
+    def ring_total(zc, n):
+        for way in range(2):
+            ring[way, 4, zc, n].wait_recv()
+        rows = cols(ring_block(j, zc, 0), BLOCK)
+        return (
+            pair[n][rows, :].astype(jnp.float32)
+            + rr[0, 3, zc, n].astype(jnp.float32)
+            + rr[1, 3, zc, n].astype(jnp.float32)
+        )
+
+    across = []
+    for n in range(2):
+        zs[n] = ring_total(1, n).astype(jnp.bfloat16)
+        across.append(push(zs.at[n], zr.at[n], send4.at[n], recv4.at[n], z_peer(i, j, h)))
+    for n, out in enumerate((sk, sv)):
+        total = ring_total(0, n)
+        across[n].wait_recv()
+        out[...] = (total + zr[n].astype(jnp.float32)).astype(jnp.bfloat16)
 
     def pieces(c):
         rows = cols(c, OWN)
@@ -354,9 +471,7 @@
     last = []
     for d in range(1, HEADS):
         for n, (src, dst) in enumerate(pieces(lax.rem(h + d, HEADS))):
-            copy = remote(src, dst, send2.at[d, n], recv2.at[d, n], head_peer(i, j, h, d))
-            copy.start()
-            last.append(copy)
+            last.append(push(src, dst, send2.at[d, n], recv2.at[d, n], head_peer(i, j, h, d)))
     own = []
     for n, (src, dst) in enumerate(pieces(h)):
         copy = pltpu.make_async_copy(src, dst, local_sem.at[n])
@@ -366,7 +481,7 @@
         copy.wait()
     for copy in last:
         copy.wait_recv()
-    for copy in pairs + query_parts + last:
+    for copy in sent:
         copy.wait_send()
 
 
@@ -384,8 +499,10 @@
         out_specs=[VMEM] * 3,
         scratch_shapes=[
             pltpu.VMEM((NX - 1, BLOCK, GROUP * WIDTH), bf16),
-            pltpu.VMEM((NJ - 1, BLOCK, WIDTH), bf16),
-            pltpu.VMEM((NJ - 1, BLOCK, WIDTH), bf16),
+            pltpu.VMEM((2, 4, 2, 2, BLOCK, WIDTH), bf16),
+            pltpu.VMEM((2, 3, 2, 2, BLOCK, WIDTH), bf16),
+            pltpu.VMEM((2, BLOCK, WIDTH), bf16),
+            pltpu.VMEM((2, BLOCK, WIDTH), bf16),
             pltpu.VMEM((BLOCK, GROUP * WIDTH), bf16),
             pltpu.VMEM((BLOCK, WIDTH), bf16),
             pltpu.VMEM((BLOCK, WIDTH), bf16),
@@ -394,8 +511,10 @@
             dma((NX,)),
             dma((HEADS, 3)),
             dma((HEADS, 3)),
-            dma((NJ, 2)),
-            dma((NJ, 2)),
+            dma((2, 4, 2, 2)),
+            dma((2, 4, 2, 2)),
+            dma((2,)),
+            dma((2,)),
         ],
         compiler_params=pltpu.CompilerParams(collective_id=2, has_side_effects=True),
         name="scatter",
@@ -418,13 +537,9 @@
     qa, ga, ka, va, ea = gather(
         queries, output_gradient, keys, values, extra.reshape(KEY_VALUE_HEADS * 8, 128)
     )
-    extra_all = ea.reshape(NX, HEADS, 8, 128)[..., :OWN].transpose(2, 0, 1, 3).reshape(8, QT)
-    query_spans = lax.dynamic_index_in_dim(span_order.reshape(NX, NJ, 2), j, 1, keepdims=False)
-    qpos = (query_spans.reshape(-1, 1) * CH + jnp.arange(CH, dtype=jnp.int32)).reshape(1, QT)
-    spans = lax.dynamic_slice_in_dim(span_order, i * (KT // CH), KT // CH)
-    own_stats = stats(spans, qpos, qa, ka)
+    own_stats = stats(span_order, qa, ka)
     all_stats = share(own_stats)
-    dq, dk, dv = grads(spans, qpos, all_stats, extra_all, qa, ga, ka, va)
+    dq, dk, dv = grads(span_order, all_stats, ea, qa, ga, ka, va)
     return scatter(dq, dk, dv)
 
 

time: 138 us -> 113 us (0.82)
  Pallas kernels: 127 us -> 106 us
  local copies, waits for them, and re-layouts: 7.8 us -> 4.63 us
    pallas_call x1, Pallas kernels: 45.7 us -> 34.8 us  [scatter(): pl.pallas_call(scatter_kernel, out_shape=(jax.ShapeDtypeStruct((OWN, QUER...]
    pallas_call x1, Pallas kernels: 50.9 us -> 40.8 us  [gather(): pl.pallas_call(gather_kernel, out_shape=shapes, in_specs=[VMEM] * 5, out_...]
    unnamed x13 -> x10, local copies, waits for them, and re-layouts: 4.66 us -> 3.62 us
where the time goes in v2:
time: 113 us
  Pallas kernels  106 us (94%)
  local copies, waits for them, and re-layouts  4.63 us (4%)
  other arithmetic  1.21 us (1%)
    pallas_call x1, Pallas kernels, gather(): pl.pallas_call(gather_kernel, out_shape=shapes, in_specs=[VMEM] * 5, out_...  40.8 us
    pallas_call x1, Pallas kernels, scatter(): pl.pallas_call(scatter_kernel, out_shape=(jax.ShapeDtypeStruct((OWN, QUER...  34.8 us
    pallas_call x1, Pallas kernels, grads(): pl.pallas_call(grads_kernel, out_shape=(jax.ShapeDtypeStruct((QT, GROUP *...  16.1 us
    pallas_call x1, Pallas kernels, stats(): pl.pallas_call(stats_kernel, out_shape=jax.ShapeDtypeStruct((2 * GROUP, Q...  7.44 us
    pallas_call x1, Pallas kernels, share(): pl.pallas_call(share_kernel, out_shape=jax.ShapeDtypeStruct((NX * 2 * GRO...  7.11 us
    unnamed x10, local copies, waits for them, and re-layouts  3.62 us

profile of v2, /device:TPU:1, one launch (start us, length us, event | category | flops | bytes accessed | tf_op | source)
XLA Modules:
  0.0 112.7 jit_solution(14527175442754535403)
XLA Ops:
  0.6 0.0 copy-start.2
  0.6 0.6 copy-done.2
  1.3 0.1 dynamic_slice.3
  1.4 1.0 convert_multiply_fusion
  2.4 0.2 reshape.12
  2.6 0.2 reduce_sum.9
  2.8 0.1 copy.11
  2.9 0.6 pad_bitcast_fusion.e_ref
  3.6 40.8 %gather.1 = (bf16[512,512]{1,0:T(8,128)(2,1)}, bf16[512,512]{1,0:T(8,128)(2,1)}, bf16[2048,128]{1,0:T(8,128)(2,1)}, bf16[2048,128]{1,0:T(8,128)(2,1)}, f32[32,128]{1,0:T(8,128)}) custom-call(bf16[16,4096]{1,0:T(8,128)(2,1)} %q_ref.1, bf16[16,4096]{1,0:T(8,128)(2,1)} %g_ref.1, bf16[16,1024]{1,0:T(8,128)(2,1)} %k_ref.1, bf16[16,1024]{1,0:T(8,128)(2,1)} %v_ref.1, ...), custom_call_target="tpu_custom_call" | custom-call | tf_op jit(solution)/shard_map/gather/pallas_call | solution.py:205
  44.3 7.4 %stats.1.in_ref = f32[8,512]{1,0:T(8,128)} custom-call(s32[128]{0:T(128)} %spans.3, bf16[512,512]{1,0:T(8,128)(2,1)} %get-tuple-element.11.q_ref, bf16[2048,128]{1,0:T(8,128)(2,1)} %get-tuple-element.12.k_ref), custom_call_target="tpu_custom_call" | custom-call | tf_op jit(solution)/shard_map/stats/pallas_call | solution.py:285
  51.7 7.1 %share.1.stats_ref = f32[32,512]{1,0:T(8,128)} custom-call(f32[8,512]{1,0:T(8,128)} %stats.1.in_ref), custom_call_target="tpu_custom_call" | custom-call | tf_op jit(solution)/shard_map/share/pallas_call | solution.py:314
  58.9 16.1 %grads.1 = (bf16[512,512]{1,0:T(8,128)(2,1)}, bf16[2048,128]{1,0:T(8,128)(2,1)}, bf16[2048,128]{1,0:T(8,128)(2,1)}) custom-call(s32[128]{0:T(128)} %spans.3, f32[32,512]{1,0:T(8,128)} %share.1.stats_ref, f32[32,128]{1,0:T(8,128)} %get-tuple-element.13.extra_ref, bf16[512,512]{1,0:T(8,128)(2,1)} %get-tuple-element.11.q_ref, ...), custom_call_target="tpu_custom_call" | custom-call | tf_op jit(solution)/shard_map/grads/pallas_call | solution.py:374
  75.0 34.8 %scatter.1 = (bf16[16,4096]{1,0:T(8,128)(2,1)}, bf16[16,1024]{1,0:T(8,128)(2,1)}, bf16[16,1024]{1,0:T(8,128)(2,1)}) custom-call(bf16[512,512]{1,0:T(8,128)(2,1)} %get-tuple-element.16.dq_ref, bf16[2048,128]{1,0:T(8,128)(2,1)} %get-tuple-element.17.dk_ref, bf16[2048,128]{1,0:T(8,128)(2,1)} %get-tuple-element.18.dv_ref), custom_call_target="tpu_custom_call" | custom-call | tf_op jit(solution)/shard_map/scatter/pallas_call | solution.py:491
  109.8 0.0 copy-start.1
  109.8 1.6 %copy.17 = bf16[16,4096]{1,0:T(8,128)(2,1)} copy(bf16[16,4096]{1,0:T(8,128)(2,1)} %get-tuple-element.22) | data formatting | bytes 262144
  111.4 0.0 copy-done.1
  111.4 0.0 copy-start
  111.4 0.6 copy.18
  112.0 0.2 copy-done
  112.1 0.6 copy.19
  (4 shorter events, 0.0 us)
Async XLA Ops:
  0.6 0.7 copy-start.2
  109.8 1.6 %copy-start.1 = (bf16[16,1024]{1,0:T(8,128)(2,1)S(1)}, bf16[16,1024]{1,0:T(8,128)(2,1)}, u32[]{:S(2)}) copy-start(bf16[16,1024]{1,0:T(8,128)(2,1)} %get-tuple-element.23) | copy-start | bytes 98308
  111.4 0.8 copy-start

commit v3 on v1

v3 whole, which is shorter than its diff:
```python
import functools
import math

import jax
import jax.numpy as jnp
from jax import lax
from jax.experimental import pallas as pl
from jax.experimental.pallas import tpu as pltpu
from jax.sharding import PartitionSpec as P

QUERY_HEADS = 32
KEY_VALUE_HEADS = 8
GROUP = 4
WIDTH = 128
CH = 64
HEADS = 8
NX = 4
NJ = 16
NY = 8
OWN = 16
BLOCK = 128
QT = NX * BLOCK
KT = NJ * BLOCK
KB = 512
SCALE = 1.0 / math.sqrt(WIDTH)
SCALE2 = SCALE * math.log2(math.e)
LOW = -1e30
FLOOR = -1e20

MESH = pl.DeviceIdType.MESH
VMEM = pl.BlockSpec(memory_space=pltpu.VMEM)
SMEM = pl.BlockSpec(memory_space=pltpu.SMEM)
NT = (((1,), (1,)), ((), ()))
TN = (((0,), (0,)), ((), ()))


def place():
    ctx = lax.axis_index("ctx")
    return ctx // NJ, lax.rem(ctx, NJ), lax.axis_index("head")


def head_peer(i, j, h, d):
    return {"ctx": i * NJ + j, "head": lax.rem(h + d, HEADS)}


def x_peer(i, j, h, d):
    return {"ctx": lax.rem(i + d, NX) * NJ + j, "head": h}


def greet(peers):
    barrier = pltpu.get_barrier_semaphore()
    for peer in peers:
        pl.semaphore_signal(barrier, inc=1, device_id=peer, device_id_type=MESH)
    pl.semaphore_wait(barrier, len(peers))


def remote(src, dst, send, recv, peer):
    return pltpu.make_async_remote_copy(
        src_ref=src, dst_ref=dst, send_sem=send, recv_sem=recv, device_id=peer, device_id_type=MESH
    )


def cols(index, width):
    return pl.ds(pl.multiple_of(index * width, width), width)


def z_peer(i, j, h):
    return {"ctx": i * NJ + lax.rem(j + NY, NJ), "head": h}


def y_peer(i, j, h, d):
    return {"ctx": i * NJ + (j // NY) * NY + lax.rem(lax.rem(j, NY) + d + NY, NY), "head": h}


def ring_block(j, zc, d):
    other = lax.rem(j // NY + zc, 2)
    return other * NY + lax.rem(lax.rem(j, NY) + d + 2 * NY, NY)


def all_peers(i, j, h):
    return (
        [head_peer(i, j, h, d) for d in range(1, HEADS)]
        + [x_peer(i, j, h, d) for d in range(1, NX)]
        + [z_peer(i, j, h), y_peer(i, j, h, 1), y_peer(i, j, h, -1)]
    )


def query_positions(spans):
    i, j, h = place()
    lane = lax.broadcasted_iota(jnp.int32, (1, BLOCK), 1)
    rows = []
    for x in range(NX):
        at = 2 * (x * NJ + j)
        start = jnp.where(lane < CH, spans[at] * CH, spans[at + 1] * CH - CH)
        rows.append(start + lane)
    return jnp.concatenate(rows, axis=1)


def extra_row(extra_ref, n):
    return jnp.concatenate([extra_ref[8 * x + n : 8 * x + n + 1, :] for x in range(NX)], axis=1)


def masked_scores(spans, starts, qpos, key_block, query_head):
    scores = lax.dot_general(key_block, query_head, NT, preferred_element_type=jnp.float32)
    row = lax.broadcasted_iota(jnp.int32, (CH, QT), 0) - qpos
    parts = [
        jnp.where(row <= -CH * spans[at], scores[n * CH : (n + 1) * CH], LOW)
        for n, at in enumerate(starts)
    ]
    return jnp.concatenate(parts, axis=0)


def attention_kernel(
    spans, q_ref, g_ref, k_ref, v_ref, e_ref, oq, ok, ov,
    qa, ga, ka, va, ea, ep, st, sa, acc, dq, dk, dv, rq, rr, run, zs, zr, sq, sk, sv,
    local_sem, send1, recv1, send2, recv2, send3, recv3, send4, recv4, send5, recv5,
    send6, recv6, send7, recv7, send8, recv8, send9, recv9, out_sem, send10, recv10,
):
    i, j, h = place()
    zh, core = h // 2, lax.rem(h, 2)
    greet(all_peers(i, j, h))
    sent = []

    def push(src, dst, send, recv, peer):
        copy = remote(src, dst, send, recv, peer)
        copy.start()
        sent.append(copy)
        return copy

    ways = (1, -1)
    x_ways = (1, NX - 1)

    near_first = (1, 2, 3, 6, 7, 4, 5)

    def rank(at):
        return lax.rem(zh + at // 2, 4) * 2 + lax.rem(core + at % 2, 2)

    def pieces(c):
        mine_q = cols(i * HEADS + h, OWN)
        mine_k = cols(j * HEADS + h, OWN)
        return [
            (k_ref.at[:, cols(c, WIDTH)], ka.at[mine_k, :]),
            (v_ref.at[:, cols(c, WIDTH)], va.at[mine_k, :]),
            (e_ref.at[cols(c, 8), :], ep.at[cols(h, 8), :]),
            (q_ref.at[:, cols(c, GROUP * WIDTH)], qa.at[mine_q, :]),
            (g_ref.at[:, cols(c, GROUP * WIDTH)], ga.at[mine_q, :]),
        ]

    first = {}
    for kinds in ((0, 1), (2, 3, 4)):
        for at in near_first:
            c = rank(at)
            for n in kinds:
                src, dst = pieces(c)[n]
                peer = {"ctx": i * NJ + j, "head": c}
                first[at, n] = push(src, dst, send1.at[at, n], recv1.at[at, n], peer)
    own = []
    for n, (src, dst) in enumerate(pieces(h)):
        copy = pltpu.make_async_copy(src, dst, local_sem.at[n])
        copy.start()
        own.append(copy)
    for copy in own:
        copy.wait()

    pair = (ka, va)
    ring = {}

    def spread(ref, rows, send, recv, peer):
        return push(ref.at[rows, :], ref.at[rows, :], send, recv, peer)

    def ring_push(step, zc, way, kinds):
        rows = cols(ring_block(j, zc, -ways[way] * (step - 1)), BLOCK)
        for n in kinds:
            at = (way, step - 1, zc, n)
            ring[way, step, zc, n] = spread(
                pair[n], rows, send3.at[at], recv3.at[at], y_peer(i, j, h, ways[way])
            )

    def ring_step(step):
        for zc in range(2):
            for way in range(2):
                for n in range(2):
                    ring[way, step - 1, zc, n].wait_recv()
                ring_push(step, zc, way, (0, 1) if step < 4 else (way,))

    x_first, x_last = {}, {}

    def x_start(dz):
        for dc in range(2):
            if dz or dc:
                for n in (3, 4):
                    first[2 * dz + dc, n].wait_recv()
        rows = cols(i * 4 + lax.rem(zh - dz + 4, 4), 2 * OWN)
        for way in range(2):
            for n, ref in enumerate((qa, ga)):
                at = (way, 0, n, dz)
                x_first[way, n, dz] = spread(
                    ref, rows, send2.at[at], recv2.at[at], x_peer(i, j, h, x_ways[way])
                )

    def x_relay(dz):
        for way, ref in enumerate((qa, ga)):
            x_first[way, way, dz].wait_recv()
            x = lax.rem(i - ways[way] + NX, NX)
            rows = cols(x * 4 + lax.rem(zh - dz + 4, 4), 2 * OWN)
            at = (way, 1, way, dz)
            x_last[way, dz] = spread(
                ref, rows, send2.at[at], recv2.at[at], x_peer(i, j, h, x_ways[way])
            )

    for n in range(2):
        for at in near_first:
            first[at, n].wait_recv()
    across = [
        spread(pair[n], cols(j, BLOCK), send4.at[n], recv4.at[n], z_peer(i, j, h))
        for n in range(2)
    ]
    for way in range(2):
        ring_push(1, 0, way, (0, 1))
    x_start(0)
    for copy in across:
        copy.wait_recv()
    for way in range(2):
        ring_push(1, 1, way, (0, 1))
    x_start(1)
    x_start(3)
    ring_step(2)
    x_relay(0)
    x_start(2)
    for at in near_first:
        first[at, 2].wait_recv()
    ea[cols(i, 8), :] = jnp.concatenate(
        [ep[8 * n : 8 * n + 8, :OWN] for n in range(HEADS)], axis=1
    )
    extras = [
        spread(ea, cols(i, 8), send5.at[d], recv5.at[d], x_peer(i, j, h, d)) for d in range(1, NX)
    ]
    ring_step(3)
    x_relay(1)
    x_relay(3)
    ring_step(4)
    x_relay(2)
    for zc in range(2):
        for way in range(2):
            ring[way, 4, zc, way].wait_recv()
    for dz in range(4):
        for way in range(2):
            x_first[way, 1 - way, dz].wait_recv()
            x_last[way, dz].wait_recv()
    for copy in extras:
        copy.wait_recv()

    qpos = query_positions(spans)
    first_span = i * (KT // CH)

    def stats_step(b, carry):
        key_block = ka[pl.ds(pl.multiple_of(b * KB, KB), KB), :]
        starts = [first_span + b * (KB // CH) + n for n in range(KB // CH)]
        following = []
        for g in range(GROUP):
            top, total = carry[g]
            scores = masked_scores(
                spans, starts, qpos, key_block, qa[:, g * WIDTH : (g + 1) * WIDTH]
            )
            new_top = jnp.maximum(top, jnp.max(scores, axis=0, keepdims=True))
            total = total * jnp.exp2((top - new_top) * SCALE2) + jnp.sum(
                jnp.exp2((scores - new_top) * SCALE2), axis=0, keepdims=True
            )
            following.append((new_top, total))
        return tuple(following)

    start = tuple(
        (jnp.full((1, QT), FLOOR, jnp.float32), jnp.zeros((1, QT), jnp.float32))
        for g in range(GROUP)
    )
    result = lax.fori_loop(0, KT // KB, stats_step, start)
    st[...] = jnp.concatenate([r[0] for r in result] + [r[1] for r in result], axis=0)
    shared = [
        push(st, sa.at[d - 1], send6.at[d], recv6.at[d], x_peer(i, j, h, d)) for d in range(1, NX)
    ]
    gain = extra_row(ea, GROUP)
    gain_scale = gain * SCALE
    out_dots = [extra_row(ea, g) for g in range(GROUP)]
    acc[...] = jnp.zeros_like(acc)
    for copy in shared:
        copy.wait_recv()
    blocks = [st[...]] + [sa[d] for d in range(NX - 1)]
    top = functools.reduce(jnp.maximum, [b[:GROUP] for b in blocks])
    total = sum(b[GROUP:] * jnp.exp2((b[:GROUP] - top) * SCALE2) for b in blocks)
    norm_rows = top * SCALE2 + jnp.log2(total)
    norms = [norm_rows[g : g + 1] for g in range(GROUP)]

    def grads_of(d):
        owners = [ring_block(j, zc, d) for zc in range(2)]
        rows = [cols(owner, BLOCK) for owner in owners]
        key_block = jnp.concatenate([ka[r, :] for r in rows], axis=0)
        value_block = jnp.concatenate([va[r, :] for r in rows], axis=0)
        starts = [first_span + owner * 2 + n for owner in owners for n in range(2)]
        key_grad = jnp.zeros((2 * BLOCK, WIDTH), jnp.float32)
        value_grad = jnp.zeros((2 * BLOCK, WIDTH), jnp.float32)
        for g in range(GROUP):
            part = slice(g * WIDTH, (g + 1) * WIDTH)
            query_head = qa[:, part]
            grad_head = ga[:, part]
            scores = masked_scores(spans, starts, qpos, key_block, query_head)
            probs = jnp.exp2(scores * SCALE2 - norms[g])
            prob_grads = lax.dot_general(
                value_block, grad_head, NT, preferred_element_type=jnp.float32
            )
            weighted = (probs * gain).astype(jnp.bfloat16)
            score_grads = (probs * ((prob_grads - out_dots[g]) * gain_scale)).astype(jnp.bfloat16)
            key_grad += jnp.dot(score_grads, query_head, preferred_element_type=jnp.float32)
            value_grad += jnp.dot(weighted, grad_head, preferred_element_type=jnp.float32)
            acc[:, part] += lax.dot_general(
                score_grads, key_block, TN, preferred_element_type=jnp.float32
            )
        for zc in range(2):
            dk[rows[zc], :] = key_grad[zc * BLOCK : (zc + 1) * BLOCK].astype(jnp.bfloat16)
            dv[rows[zc], :] = value_grad[zc * BLOCK : (zc + 1) * BLOCK].astype(jnp.bfloat16)

    partial = (dk, dv)
    back = {}

    def back_push(src, way, step, zc, n):
        at = (way, step - 1, zc, n)
        back[way, step, zc, n] = push(
            src, rr.at[at], send7.at[at], recv7.at[at], y_peer(i, j, h, ways[way])
        )

    def target(way, step, zc):
        return cols(ring_block(j, zc, ways[way] * (5 - step)), BLOCK)

    def back_step(way, step):
        for zc in (1, 0):
            if step == 2:
                src = partial[1 - way].at[target(way, 2, zc), :]
                back_push(src, way, 2, zc, 1 - way)
            for n in range(2) if step > 2 else (way,):
                back[way, step - 1, zc, n].wait_recv()
                total = rr[way, step - 2, zc, n].astype(jnp.float32) + partial[n][
                    target(way, step, zc), :
                ].astype(jnp.float32)
                run[way, step - 2, zc, n] = total.astype(jnp.bfloat16)
                back_push(run.at[way, step - 2, zc, n], way, step, zc, n)

    grads_of(4)
    for zc in (1, 0):
        for way in range(2):
            back_push(partial[way].at[target(way, 1, zc), :], way, 1, zc, way)
    for step in range(2, 5):
        for way in range(2):
            grads_of(ways[way] * (5 - step))
            back_step(way, step)
    grads_of(0)
    dq[...] = acc[...].astype(jnp.bfloat16)
    query_parts = []
    for d in range(1, NX):
        rows = cols(lax.rem(i + d, NX), BLOCK)
        query_parts.append(
            push(dq.at[rows, :], rq.at[d - 1], send8.at[d], recv8.at[d], x_peer(i, j, h, d))
        )

    def ring_total(zc, n):
        for way in range(2):
            back[way, 4, zc, n].wait_recv()
        rows = cols(ring_block(j, zc, 0), BLOCK)
        return (
            partial[n][rows, :].astype(jnp.float32)
            + rr[0, 3, zc, n].astype(jnp.float32)
            + rr[1, 3, zc, n].astype(jnp.float32)
        )

    over = []
    for n in range(2):
        zs[n] = ring_total(1, n).astype(jnp.bfloat16)
        over.append(push(zs.at[n], zr.at[n], send9.at[n], recv9.at[n], z_peer(i, j, h)))
    for n, out in enumerate((sk, sv)):
        total = ring_total(0, n)
        over[n].wait_recv()
        out[...] = (total + zr[n].astype(jnp.float32)).astype(jnp.bfloat16)

    def finished(c):
        rows = cols(c, OWN)
        return [
            (sk.at[rows, :], ok.at[:, cols(h, WIDTH)]),
            (sv.at[rows, :], ov.at[:, cols(h, WIDTH)]),
            (sq.at[rows, :], oq.at[:, cols(h, GROUP * WIDTH)]),
        ]

    last = []

    def give(kinds):
        for at in (4, 5, 2, 3, 6, 7, 1):
            c = rank(at)
            for n in kinds:
                src, dst = finished(c)[n]
                peer = {"ctx": i * NJ + j, "head": c}
                last.append(push(src, dst, send10.at[at, n], recv10.at[at, n], peer))
        for n in kinds:
            src, dst = finished(h)[n]
            copy = pltpu.make_async_copy(src, dst, out_sem.at[n])
            copy.start()
            kept.append(copy)

    kept = []
    give((0, 1))
    for copy in query_parts:
        copy.wait_recv()
    total = dq[cols(i, BLOCK), :].astype(jnp.float32)
    for d in range(1, NX):
        total += rq[d - 1].astype(jnp.float32)
    sq[...] = total.astype(jnp.bfloat16)
    give((2,))
    for copy in kept:
        copy.wait()
    for copy in last:
        copy.wait_recv()
    for copy in sent:
        copy.wait_send()


def attention(spans, queries, grads, keys, values, extra):
    dma = pltpu.SemaphoreType.DMA
    bf16, f32 = jnp.bfloat16, jnp.float32
    vmem = pltpu.VMEM

    def both(*shape):
        return [dma(shape), dma(shape)]

    return pl.pallas_call(
        attention_kernel,
        out_shape=(
            jax.ShapeDtypeStruct((OWN, QUERY_HEADS * WIDTH), bf16),
            jax.ShapeDtypeStruct((OWN, KEY_VALUE_HEADS * WIDTH), bf16),
            jax.ShapeDtypeStruct((OWN, KEY_VALUE_HEADS * WIDTH), bf16),
        ),
        in_specs=[SMEM] + [VMEM] * 5,
        out_specs=[VMEM] * 3,
        scratch_shapes=[
            vmem((QT, GROUP * WIDTH), bf16),
            vmem((QT, GROUP * WIDTH), bf16),
            vmem((KT, WIDTH), bf16),
            vmem((KT, WIDTH), bf16),
            vmem((NX * 8, 128), f32),
            vmem((HEADS * 8, 128), f32),
            vmem((2 * GROUP, QT), f32),
            vmem((NX - 1, 2 * GROUP, QT), f32),
            vmem((QT, GROUP * WIDTH), f32),
            vmem((QT, GROUP * WIDTH), bf16),
            vmem((KT, WIDTH), bf16),
            vmem((KT, WIDTH), bf16),
            vmem((NX - 1, BLOCK, GROUP * WIDTH), bf16),
            vmem((2, 4, 2, 2, BLOCK, WIDTH), bf16),
            vmem((2, 3, 2, 2, BLOCK, WIDTH), bf16),
            vmem((2, BLOCK, WIDTH), bf16),
            vmem((2, BLOCK, WIDTH), bf16),
            vmem((BLOCK, GROUP * WIDTH), bf16),
            vmem((BLOCK, WIDTH), bf16),
            vmem((BLOCK, WIDTH), bf16),
            dma((5,)),
        ]
        + both(HEADS, 5)
        + both(2, 2, 2, 4)
        + both(2, 4, 2, 2)
        + both(2)
        + both(NX)
        + both(NX)
        + both(2, 4, 2, 2)
        + both(NX)
        + both(2)
        + [dma((3,))]
        + both(HEADS, 3),
        compiler_params=pltpu.CompilerParams(collective_id=0, has_side_effects=True),
        name="attention",
    )(spans, queries, grads, keys, values, extra)


def on_device(queries, keys, values, outputs, output_gradient, importance, span_order):
    i, j, h = place()
    out_dot = jnp.sum(
        (output_gradient.astype(jnp.float32) * outputs.astype(jnp.float32)).reshape(
            OWN, KEY_VALUE_HEADS, GROUP, WIDTH
        ),
        axis=-1,
    ).transpose(1, 2, 0)
    own_gain = lax.dynamic_slice_in_dim(importance.astype(jnp.float32) * 0.25, h * OWN, OWN)
    extra = jnp.concatenate(
        [out_dot, jnp.broadcast_to(own_gain, (KEY_VALUE_HEADS, 1, OWN))], axis=1
    )
    extra = jnp.pad(extra, ((0, 0), (0, 8 - GROUP - 1), (0, 128 - OWN)))
    return attention(
        span_order, queries, output_gradient, keys, values, extra.reshape(KEY_VALUE_HEADS * 8, 128)
    )


def solution(mesh):
    tokens = P(("ctx", "head"), None)
    return jax.shard_map(
        on_device,
        mesh=mesh,
        in_specs=(tokens, tokens, tokens, tokens, tokens, P("ctx"), P()),
        out_specs=(tokens, tokens, tokens),
        check_vma=False,
    )
```

time: 138 us -> 93 us (0.67)
  Pallas kernels: 127 us -> 86.2 us
  local copies, waits for them, and re-layouts: 7.8 us -> 4.63 us
    pallas_call x5 -> x1, Pallas kernels: 127 us -> 86.2 us  [attention(): pl.pallas_call(attention_kernel, out_shape=(jax.ShapeDtypeStruct((OWN, QU...]
    unnamed x13 -> x10, local copies, waits for them, and re-layouts: 4.66 us -> 3.62 us
where the time goes in v3:
time: 93 us; the launch traced here: 92.7 us
  Pallas kernels  86.2 us (93%)
  local copies, waits for them, and re-layouts  4.63 us (5%)
  other arithmetic  1.21 us (1%)
    pallas_call x1, Pallas kernels, attention(): pl.pallas_call(attention_kernel, out_shape=(jax.ShapeDtypeStruct((OWN, QU...  86.2 us
    unnamed x10, local copies, waits for them, and re-layouts  3.62 us

profile of v3, /device:TPU:1, one launch (start us, length us, event | category | flops | bytes accessed | tf_op | source)
XLA Modules:
  0.0 92.7 jit_solution(17130170742969549745)
XLA Ops:
  0.6 0.0 copy-start.2
  0.6 0.6 copy-done.2
  1.3 0.1 dynamic_slice.3
  1.4 1.0 %convert_multiply_fusion = f32[16,4096]{1,0:T(8,128)S(1)} fusion(bf16[16,4096]{1,0:T(8,128)(2,1)} %param.10, bf16[16,4096]{1,0:T(8,128)(2,1)} %g_ref.1), kind=kLoop, calls=%fused_computation | loop fusion | flops 196608 | bytes 524288 | tf_op jit(solution)/shard_map/mul | solution.py:481
  2.4 0.2 reshape.12
  2.6 0.2 reduce_sum.9
  2.8 0.1 copy.11
  2.9 0.6 pad_bitcast_fusion.e_ref
  3.6 86.2 %attention.1 = (bf16[16,4096]{1,0:T(8,128)(2,1)}, bf16[16,1024]{1,0:T(8,128)(2,1)}, bf16[16,1024]{1,0:T(8,128)(2,1)}) custom-call(s32[128]{0:T(128)} %spans.1, bf16[16,4096]{1,0:T(8,128)(2,1)} %q_ref.1, bf16[16,4096]{1,0:T(8,128)(2,1)} %g_ref.1, bf16[16,1024]{1,0:T(8,128)(2,1)} %k_ref.1, bf16[16,1024]{1,0:T(8,128)(2,1)} %v_ref.1, ...), custom_call_target="tpu_custom_call" | custom-call | tf_op jit(solution)/shard_map/attention/pallas_call | solution.py:430
  89.7 0.0 copy-start.1
  89.8 1.6 %copy.17 = bf16[16,4096]{1,0:T(8,128)(2,1)} copy(bf16[16,4096]{1,0:T(8,128)(2,1)} %get-tuple-element.6) | data formatting | bytes 262144
  91.3 0.0 copy-done.1
  91.3 0.0 copy-start
  91.3 0.6 copy.18
  91.9 0.2 copy-done
  92.1 0.6 copy.19
  (4 shorter events, 0.0 us)
Async XLA Ops:
  0.6 0.7 copy-start.2
  89.7 1.6 %copy-start.1 = (bf16[16,1024]{1,0:T(8,128)(2,1)S(1)}, bf16[16,1024]{1,0:T(8,128)(2,1)}, u32[]{:S(2)}) copy-start(bf16[16,1024]{1,0:T(8,128)(2,1)} %get-tuple-element.7) | copy-start | bytes 98308
  91.3 0.8 copy-start

commit v4 on v3

--- a/solution.py
+++ b/solution.py
@@ -47,11 +47,11 @@
     return {"ctx": lax.rem(i + d, NX) * NJ + j, "head": h}
 
 
-def greet(peers):
-    barrier = pltpu.get_barrier_semaphore()
+def announce(peers):
     for peer in peers:
-        pl.semaphore_signal(barrier, inc=1, device_id=peer, device_id_type=MESH)
-    pl.semaphore_wait(barrier, len(peers))
+        pl.semaphore_signal(
+            pltpu.get_barrier_semaphore(), inc=1, device_id=peer, device_id_type=MESH
+        )
 
 
 def remote(src, dst, send, recv, peer):
@@ -85,15 +85,10 @@
     )
 
 
-def query_positions(spans):
-    i, j, h = place()
+def block_positions(spans, x, j):
     lane = lax.broadcasted_iota(jnp.int32, (1, BLOCK), 1)
-    rows = []
-    for x in range(NX):
-        at = 2 * (x * NJ + j)
-        start = jnp.where(lane < CH, spans[at] * CH, spans[at + 1] * CH - CH)
-        rows.append(start + lane)
-    return jnp.concatenate(rows, axis=1)
+    at = 2 * (x * NJ + j)
+    return jnp.where(lane < CH, spans[at] * CH, spans[at + 1] * CH - CH) + lane
 
 
 def extra_row(extra_ref, n):
@@ -111,14 +106,28 @@
 
 
 def attention_kernel(
-    spans, q_ref, g_ref, k_ref, v_ref, e_ref, oq, ok, ov,
-    qa, ga, ka, va, ea, ep, st, sa, acc, dq, dk, dv, rq, rr, run, zs, zr, sq, sk, sv,
+    spans, q_ref, g_ref, k_ref, v_ref, o_ref, w_ref, oq, ok, ov,
+    e_ref, qa, ga, ka, va, ea, ep, st, sa, acc, dq, dk, dv, rq, rr, run, zs, zr, sq, sk, sv,
     local_sem, send1, recv1, send2, recv2, send3, recv3, send4, recv4, send5, recv5,
     send6, recv6, send7, recv7, send8, recv8, send9, recv9, out_sem, send10, recv10,
 ):
     i, j, h = place()
     zh, core = h // 2, lax.rem(h, 2)
-    greet(all_peers(i, j, h))
+    peers = all_peers(i, j, h)
+    announce(peers)
+
+    lane_head = lax.broadcasted_iota(jnp.int32, (8, GROUP * WIDTH), 1) // WIDTH
+    pick = (lane_head == lax.broadcasted_iota(jnp.int32, (8, GROUP * WIDTH), 0)).astype(jnp.float32)
+    for c in range(KEY_VALUE_HEADS):
+        part = slice(c * GROUP * WIDTH, (c + 1) * GROUP * WIDTH)
+        product = g_ref[:, part].astype(jnp.float32) * o_ref[:, part].astype(jnp.float32)
+        sums = lax.dot_general(
+            pick, product, NT, precision=lax.Precision.HIGHEST, preferred_element_type=jnp.float32
+        )
+        e_ref[8 * c : 8 * c + 8, :] = jnp.concatenate(
+            [sums, jnp.zeros((8, 128 - OWN), jnp.float32)], axis=1
+        )
+    pl.semaphore_wait(pltpu.get_barrier_semaphore(), len(peers))
     sent = []
 
     def push(src, dst, send, recv, peer):
@@ -229,9 +238,10 @@
     x_start(2)
     for at in near_first:
         first[at, 2].wait_recv()
-    ea[cols(i, 8), :] = jnp.concatenate(
-        [ep[8 * n : 8 * n + 8, :OWN] for n in range(HEADS)], axis=1
-    )
+    own_extra = jnp.concatenate([ep[8 * n : 8 * n + 8, :OWN] for n in range(HEADS)], axis=1)
+    own_gain = w_ref[...].astype(jnp.float32) * 0.25
+    extra_at = lax.broadcasted_iota(jnp.int32, (8, BLOCK), 0)
+    ea[cols(i, 8), :] = jnp.where(extra_at == GROUP, own_gain, own_extra)
     extras = [
         spread(ea, cols(i, 8), send5.at[d], recv5.at[d], x_peer(i, j, h, d)) for d in range(1, NX)
     ]
@@ -243,41 +253,63 @@
     for zc in range(2):
         for way in range(2):
             ring[way, 4, zc, way].wait_recv()
+    first_span = i * (KT // CH)
+
+    def stats_of(x):
+        rows = cols(x, BLOCK)
+        block = jnp.concatenate(
+            [qa[rows, g * WIDTH : (g + 1) * WIDTH] for g in range(GROUP)], axis=0
+        )
+        positions = jnp.concatenate([block_positions(spans, x, j)] * GROUP, axis=1)
+
+        def merge(one, two):
+            top = jnp.maximum(one[0], two[0])
+            return top, one[1] * jnp.exp2((one[0] - top) * SCALE2) + two[1] * jnp.exp2(
+                (two[0] - top) * SCALE2
+            )
+
+        def stats_step(b, carry):
+            following = []
+            for half in range(2):
+                at = 2 * b + half
+                key_block = ka[pl.ds(pl.multiple_of(at * KB, KB), KB), :]
+                starts = [first_span + at * (KB // CH) + n for n in range(KB // CH)]
+                scores = masked_scores(spans, starts, positions, key_block, block)
+                top = jnp.maximum(FLOOR, jnp.max(scores, axis=0, keepdims=True))
+                total = jnp.sum(jnp.exp2((scores - top) * SCALE2), axis=0, keepdims=True)
+                following.append(merge(carry[half], (top, total)))
+            return tuple(following)
+
+        nothing = (
+            jnp.full((1, GROUP * BLOCK), FLOOR, jnp.float32),
+            jnp.zeros((1, GROUP * BLOCK), jnp.float32),
+        )
+        halves = lax.fori_loop(0, KT // KB // 2, stats_step, (nothing, nothing))
+        found = merge(*halves)
+        st[:, rows] = jnp.concatenate(
+            [r[:, g * BLOCK : (g + 1) * BLOCK] for r in found for g in range(GROUP)], axis=0
+        )
+
     for dz in range(4):
-        for way in range(2):
-            x_first[way, 1 - way, dz].wait_recv()
-            x_last[way, dz].wait_recv()
-    for copy in extras:
-        copy.wait_recv()
-
-    qpos = query_positions(spans)
-    first_span = i * (KT // CH)
-
-    def stats_step(b, carry):
-        key_block = ka[pl.ds(pl.multiple_of(b * KB, KB), KB), :]
-        starts = [first_span + b * (KB // CH) + n for n in range(KB // CH)]
-        following = []
-        for g in range(GROUP):
-            top, total = carry[g]
-            scores = masked_scores(
-                spans, starts, qpos, key_block, qa[:, g * WIDTH : (g + 1) * WIDTH]
-            )
-            new_top = jnp.maximum(top, jnp.max(scores, axis=0, keepdims=True))
-            total = total * jnp.exp2((top - new_top) * SCALE2) + jnp.sum(
-                jnp.exp2((scores - new_top) * SCALE2), axis=0, keepdims=True
-            )
-            following.append((new_top, total))
-        return tuple(following)
-
-    start = tuple(
-        (jnp.full((1, QT), FLOOR, jnp.float32), jnp.zeros((1, QT), jnp.float32))
-        for g in range(GROUP)
-    )
-    result = lax.fori_loop(0, KT // KB, stats_step, start)
-    st[...] = jnp.concatenate([r[0] for r in result] + [r[1] for r in result], axis=0)
+        x_first[1, 0, dz].wait_recv()
+
+    def early(t, carry):
+        stats_of(lax.rem(i + 3 + t, NX))
+        return carry
+
+    lax.fori_loop(0, 3, early, 0)
+    for dz in range(4):
+        x_last[0, dz].wait_recv()
+    stats_of(lax.rem(i + 2, NX))
     shared = [
         push(st, sa.at[d - 1], send6.at[d], recv6.at[d], x_peer(i, j, h, d)) for d in range(1, NX)
     ]
+    for dz in range(4):
+        x_first[0, 1, dz].wait_recv()
+        x_last[1, dz].wait_recv()
+    for copy in extras:
+        copy.wait_recv()
+    qpos = jnp.concatenate([block_positions(spans, x, j) for x in range(NX)], axis=1)
     gain = extra_row(ea, GROUP)
     gain_scale = gain * SCALE
     out_dots = [extra_row(ea, g) for g in range(GROUP)]
@@ -290,14 +322,16 @@
     norm_rows = top * SCALE2 + jnp.log2(total)
     norms = [norm_rows[g : g + 1] for g in range(GROUP)]
 
-    def grads_of(d):
-        owners = [ring_block(j, zc, d) for zc in range(2)]
+    query_parts = {}
+
+    def grads_of(distances, closing=False):
+        owners = [ring_block(j, zc, d) for d in distances for zc in range(2)]
         rows = [cols(owner, BLOCK) for owner in owners]
         key_block = jnp.concatenate([ka[r, :] for r in rows], axis=0)
         value_block = jnp.concatenate([va[r, :] for r in rows], axis=0)
         starts = [first_span + owner * 2 + n for owner in owners for n in range(2)]
-        key_grad = jnp.zeros((2 * BLOCK, WIDTH), jnp.float32)
-        value_grad = jnp.zeros((2 * BLOCK, WIDTH), jnp.float32)
+        key_grad = jnp.zeros((len(owners) * BLOCK, WIDTH), jnp.float32)
+        value_grad = jnp.zeros((len(owners) * BLOCK, WIDTH), jnp.float32)
         for g in range(GROUP):
             part = slice(g * WIDTH, (g + 1) * WIDTH)
             query_head = qa[:, part]
@@ -309,14 +343,26 @@
             )
             weighted = (probs * gain).astype(jnp.bfloat16)
             score_grads = (probs * ((prob_grads - out_dots[g]) * gain_scale)).astype(jnp.bfloat16)
+            query_term = lax.dot_general(
+                score_grads, key_block, TN, preferred_element_type=jnp.float32
+            )
+            if closing:
+                dq[g] = (acc[:, part] + query_term).astype(jnp.bfloat16)
+                for d in range(1, NX):
+                    query_parts[d, g] = push(
+                        dq.at[g, cols(lax.rem(i + d, NX), BLOCK), :],
+                        rq.at[d - 1, g],
+                        send8.at[d, g],
+                        recv8.at[d, g],
+                        x_peer(i, j, h, d),
+                    )
+            else:
+                acc[:, part] += query_term
             key_grad += jnp.dot(score_grads, query_head, preferred_element_type=jnp.float32)
             value_grad += jnp.dot(weighted, grad_head, preferred_element_type=jnp.float32)
-            acc[:, part] += lax.dot_general(
-                score_grads, key_block, TN, preferred_element_type=jnp.float32
-            )
-        for zc in range(2):
-            dk[rows[zc], :] = key_grad[zc * BLOCK : (zc + 1) * BLOCK].astype(jnp.bfloat16)
-            dv[rows[zc], :] = value_grad[zc * BLOCK : (zc + 1) * BLOCK].astype(jnp.bfloat16)
+        for n, r in enumerate(rows):
+            dk[r, :] = key_grad[n * BLOCK : (n + 1) * BLOCK].astype(jnp.bfloat16)
+            dv[r, :] = value_grad[n * BLOCK : (n + 1) * BLOCK].astype(jnp.bfloat16)
 
     partial = (dk, dv)
     back = {}
@@ -343,22 +389,18 @@
                 run[way, step - 2, zc, n] = total.astype(jnp.bfloat16)
                 back_push(run.at[way, step - 2, zc, n], way, step, zc, n)
 
-    grads_of(4)
+    grads_of((4,))
     for zc in (1, 0):
         for way in range(2):
             back_push(partial[way].at[target(way, 1, zc), :], way, 1, zc, way)
-    for step in range(2, 5):
+    for step in (2, 3):
         for way in range(2):
-            grads_of(ways[way] * (5 - step))
+            grads_of((ways[way] * (5 - step),))
             back_step(way, step)
-    grads_of(0)
-    dq[...] = acc[...].astype(jnp.bfloat16)
-    query_parts = []
-    for d in range(1, NX):
-        rows = cols(lax.rem(i + d, NX), BLOCK)
-        query_parts.append(
-            push(dq.at[rows, :], rq.at[d - 1], send8.at[d], recv8.at[d], x_peer(i, j, h, d))
-        )
+    grads_of((1,))
+    back_step(0, 4)
+    grads_of((-1, 0), closing=True)
+    back_step(1, 4)
 
     def ring_total(zc, n):
         for way in range(2):
@@ -370,47 +412,39 @@
             + rr[1, 3, zc, n].astype(jnp.float32)
         )
 
+    last, kept = [], []
+
+    def give(n, source, out):
+        for at in (4, 5, 2, 3, 6, 7, 1):
+            c = rank(at)
+            peer = {"ctx": i * NJ + j, "head": c}
+            src = source.at[cols(c, OWN), :]
+            last.append(push(src, out, send10.at[at, n], recv10.at[at, n], peer))
+        copy = pltpu.make_async_copy(source.at[cols(h, OWN), :], out, out_sem.at[n])
+        copy.start()
+        kept.append(copy)
+
+    def give_queries(g):
+        total = dq[g, cols(i, BLOCK), :].astype(jnp.float32)
+        for d in range(1, NX):
+            query_parts[d, g].wait_recv()
+            total += rq[d - 1, g].astype(jnp.float32)
+        sq[g] = total.astype(jnp.bfloat16)
+        give(g, sq.at[g], oq.at[:, cols(h * GROUP + g, WIDTH)])
+
+    give_queries(0)
     over = []
     for n in range(2):
         zs[n] = ring_total(1, n).astype(jnp.bfloat16)
         over.append(push(zs.at[n], zr.at[n], send9.at[n], recv9.at[n], z_peer(i, j, h)))
-    for n, out in enumerate((sk, sv)):
+    give_queries(1)
+    give_queries(2)
+    for n, (held, out) in enumerate(((sk, ok), (sv, ov))):
         total = ring_total(0, n)
         over[n].wait_recv()
-        out[...] = (total + zr[n].astype(jnp.float32)).astype(jnp.bfloat16)
-
-    def finished(c):
-        rows = cols(c, OWN)
-        return [
-            (sk.at[rows, :], ok.at[:, cols(h, WIDTH)]),
-            (sv.at[rows, :], ov.at[:, cols(h, WIDTH)]),
-            (sq.at[rows, :], oq.at[:, cols(h, GROUP * WIDTH)]),
-        ]
-
-    last = []
-
-    def give(kinds):
-        for at in (4, 5, 2, 3, 6, 7, 1):
-            c = rank(at)
-            for n in kinds:
-                src, dst = finished(c)[n]
-                peer = {"ctx": i * NJ + j, "head": c}
-                last.append(push(src, dst, send10.at[at, n], recv10.at[at, n], peer))
-        for n in kinds:
-            src, dst = finished(h)[n]
-            copy = pltpu.make_async_copy(src, dst, out_sem.at[n])
-            copy.start()
-            kept.append(copy)
-
-    kept = []
-    give((0, 1))
-    for copy in query_parts:
-        copy.wait_recv()
-    total = dq[cols(i, BLOCK), :].astype(jnp.float32)
-    for d in range(1, NX):
-        total += rq[d - 1].astype(jnp.float32)
-    sq[...] = total.astype(jnp.bfloat16)
-    give((2,))
+        held[...] = (total + zr[n].astype(jnp.float32)).astype(jnp.bfloat16)
+        give(GROUP + n, held, out.at[:, cols(h, WIDTH)])
+    give_queries(3)
     for copy in kept:
         copy.wait()
     for copy in last:
@@ -419,7 +453,7 @@
         copy.wait_send()
 
 
-def attention(spans, queries, grads, keys, values, extra):
+def attention(spans, queries, grads, keys, values, outputs, importance):
     dma = pltpu.SemaphoreType.DMA
     bf16, f32 = jnp.bfloat16, jnp.float32
     vmem = pltpu.VMEM
@@ -434,9 +468,10 @@
             jax.ShapeDtypeStruct((OWN, KEY_VALUE_HEADS * WIDTH), bf16),
             jax.ShapeDtypeStruct((OWN, KEY_VALUE_HEADS * WIDTH), bf16),
         ),
-        in_specs=[SMEM] + [VMEM] * 5,
+        in_specs=[SMEM] + [VMEM] * 6,
         out_specs=[VMEM] * 3,
         scratch_shapes=[
+            vmem((KEY_VALUE_HEADS * 8, 128), f32),
             vmem((QT, GROUP * WIDTH), bf16),
             vmem((QT, GROUP * WIDTH), bf16),
             vmem((KT, WIDTH), bf16),
@@ -446,15 +481,15 @@
             vmem((2 * GROUP, QT), f32),
             vmem((NX - 1, 2 * GROUP, QT), f32),
             vmem((QT, GROUP * WIDTH), f32),
-            vmem((QT, GROUP * WIDTH), bf16),
+            vmem((GROUP, QT, WIDTH), bf16),
             vmem((KT, WIDTH), bf16),
             vmem((KT, WIDTH), bf16),
-            vmem((NX - 1, BLOCK, GROUP * WIDTH), bf16),
+            vmem((NX - 1, GROUP, BLOCK, WIDTH), bf16),
             vmem((2, 4, 2, 2, BLOCK, WIDTH), bf16),
             vmem((2, 3, 2, 2, BLOCK, WIDTH), bf16),
             vmem((2, BLOCK, WIDTH), bf16),
             vmem((2, BLOCK, WIDTH), bf16),
-            vmem((BLOCK, GROUP * WIDTH), bf16),
+            vmem((GROUP, BLOCK, WIDTH), bf16),
             vmem((BLOCK, WIDTH), bf16),
             vmem((BLOCK, WIDTH), bf16),
             dma((5,)),
@@ -466,30 +501,18 @@
         + both(NX)
         + both(NX)
         + both(2, 4, 2, 2)
-        + both(NX)
+        + both(NX, GROUP)
         + both(2)
-        + [dma((3,))]
-        + both(HEADS, 3),
+        + [dma((GROUP + 2,))]
+        + both(HEADS, GROUP + 2),
         compiler_params=pltpu.CompilerParams(collective_id=0, has_side_effects=True),
         name="attention",
-    )(spans, queries, grads, keys, values, extra)
+    )(spans, queries, grads, keys, values, outputs, importance)
 
 
 def on_device(queries, keys, values, outputs, output_gradient, importance, span_order):
-    i, j, h = place()
-    out_dot = jnp.sum(
-        (output_gradient.astype(jnp.float32) * outputs.astype(jnp.float32)).reshape(
-            OWN, KEY_VALUE_HEADS, GROUP, WIDTH
-        ),
-        axis=-1,
-    ).transpose(1, 2, 0)
-    own_gain = lax.dynamic_slice_in_dim(importance.astype(jnp.float32) * 0.25, h * OWN, OWN)
-    extra = jnp.concatenate(
-        [out_dot, jnp.broadcast_to(own_gain, (KEY_VALUE_HEADS, 1, OWN))], axis=1
-    )
-    extra = jnp.pad(extra, ((0, 0), (0, 8 - GROUP - 1), (0, 128 - OWN)))
     return attention(
-        span_order, queries, output_gradient, keys, values, extra.reshape(KEY_VALUE_HEADS * 8, 128)
+        span_order, queries, output_gradient, keys, values, outputs, importance.reshape(1, BLOCK)
     )
 
 

time: 93 us -> 91.5 us (0.984)
  local copies, waits for them, and re-layouts: 4.63 us -> 2.96 us
  Pallas kernels: 86.2 us -> 87.6 us
  other arithmetic: 1.21 us -> 0 us
    pallas_call x1, Pallas kernels: 86.2 us -> 87.6 us  [attention(): pl.pallas_call(attention_kernel, out_shape=(jax.ShapeDtypeStruct((OWN, QU...]
    mul x2 -> x0, other arithmetic: 1 us -> none  [the longest x1 1 us: on_device(): output_gradient.astype(jnp.float32) * outputs.astype(jnp.float32)]
    unnamed x10 -> x7, local copies, waits for them, and re-layouts: 3.62 us -> 2.96 us
where the time goes in v4:
time: 91.5 us; the launch traced here: 91.3 us
  Pallas kernels  87.6 us (96%)
  local copies, waits for them, and re-layouts  2.96 us (3%)
    pallas_call x1, Pallas kernels, attention(): pl.pallas_call(attention_kernel, out_shape=(jax.ShapeDtypeStruct((OWN, QU...  87.6 us
    unnamed x7, local copies, waits for them, and re-layouts  2.96 us

profile of v4, /device:TPU:1, one launch (start us, length us, event | category | flops | bytes accessed | tf_op | source)
XLA Modules:
  0.0 91.3 jit_solution(1789941519709523975)
XLA Ops:
  0.6 87.6 %attention.1 = (bf16[16,4096]{1,0:T(8,128)(2,1)}, bf16[16,1024]{1,0:T(8,128)(2,1)}, bf16[16,1024]{1,0:T(8,128)(2,1)}) custom-call(s32[128]{0:T(128)} %spans.1, bf16[16,4096]{1,0:T(8,128)(2,1)} %q_ref.1, bf16[16,4096]{1,0:T(8,128)(2,1)} %g_ref.1, bf16[16,1024]{1,0:T(8,128)(2,1)} %k_ref.1, bf16[16,1024]{1,0:T(8,128)(2,1)} %v_ref.1, bf16[16,4096]{1,0:T(8,128)(2,1)} %o_ref.1, ...), custom_call_target="tpu_custom_call" | custom-call | tf_op jit(solution)/shard_map/attention/pallas_call | solution.py:464
  88.3 0.0 copy-start.1
  88.3 1.6 %copy.13 = bf16[16,4096]{1,0:T(8,128)(2,1)} copy(bf16[16,4096]{1,0:T(8,128)(2,1)} %get-tuple-element.6) | data formatting | bytes 262144
  89.9 0.0 copy-done.1
  89.9 0.0 copy-start
  89.9 0.6 copy.14
  90.5 0.2 copy-done
  90.6 0.6 copy.15
Async XLA Ops:
  88.3 1.6 %copy-start.1 = (bf16[16,1024]{1,0:T(8,128)(2,1)S(1)}, bf16[16,1024]{1,0:T(8,128)(2,1)}, u32[]{:S(2)}) copy-start(bf16[16,1024]{1,0:T(8,128)(2,1)} %get-tuple-element.7) | copy-start | bytes 98308
  89.9 0.8 copy-start

commit v5 on v4

--- a/solution.py
+++ b/solution.py
@@ -107,7 +107,7 @@
 
 def attention_kernel(
     spans, q_ref, g_ref, k_ref, v_ref, o_ref, w_ref, oq, ok, ov,
-    e_ref, qa, ga, ka, va, ea, ep, st, sa, acc, dq, dk, dv, rq, rr, run, zs, zr, sq, sk, sv,
+    e_ref, qa, ga, ka, va, ea, ep, st, sa, acc, dq, dk, dv, rq, xs, rr, run, zs, zr, sq, sk, sv,
     local_sem, send1, recv1, send2, recv2, send3, recv3, send4, recv4, send5, recv5,
     send6, recv6, send7, recv7, send8, recv8, send9, recv9, out_sem, send10, recv10,
 ):
@@ -231,11 +231,12 @@
         copy.wait_recv()
     for way in range(2):
         ring_push(1, 1, way, (0, 1))
+    ring_step(2)
     x_start(1)
     x_start(3)
-    ring_step(2)
+    ring_step(3)
+    x_start(2)
     x_relay(0)
-    x_start(2)
     for at in near_first:
         first[at, 2].wait_recv()
     own_extra = jnp.concatenate([ep[8 * n : 8 * n + 8, :OWN] for n in range(HEADS)], axis=1)
@@ -245,62 +246,67 @@
     extras = [
         spread(ea, cols(i, 8), send5.at[d], recv5.at[d], x_peer(i, j, h, d)) for d in range(1, NX)
     ]
-    ring_step(3)
+    ring_step(4)
     x_relay(1)
     x_relay(3)
-    ring_step(4)
     x_relay(2)
+
+    first_span = i * (KT // CH)
+    st[...] = jnp.where(
+        lax.broadcasted_iota(jnp.int32, (2 * GROUP, QT), 0) < GROUP, FLOOR, jnp.float32(0.0)
+    )
+
+    def stats_of(x, couple):
+        x_rows = cols(x, BLOCK)
+        block = jnp.concatenate(
+            [qa[x_rows, g * WIDTH : (g + 1) * WIDTH] for g in range(GROUP)], axis=0
+        )
+        positions = jnp.concatenate([block_positions(spans, x, j)] * GROUP, axis=1)
+        found = [(st[:GROUP, x_rows], st[GROUP:, x_rows])]
+        for half in range(2):
+            d = (couple + half) * (2 * half - 1)
+            owners = [ring_block(j, zc, d) for zc in range(2)]
+            key_block = jnp.concatenate([ka[cols(o, BLOCK), :] for o in owners], axis=0)
+            starts = [first_span + owner * 2 + n for owner in owners for n in range(2)]
+            scores = masked_scores(spans, starts, positions, key_block, block)
+            top = jnp.maximum(FLOOR, jnp.max(scores, axis=0, keepdims=True))
+            total = jnp.sum(jnp.exp2((scores - top) * SCALE2), axis=0, keepdims=True)
+            found.append(
+                [
+                    jnp.concatenate(
+                        [r[:, g * BLOCK : (g + 1) * BLOCK] for g in range(GROUP)], axis=0
+                    )
+                    for r in (top, total)
+                ]
+            )
+        top = functools.reduce(jnp.maximum, [r[0] for r in found])
+        st[:GROUP, x_rows] = top
+        st[GROUP:, x_rows] = sum(r[1] * jnp.exp2((r[0] - top) * SCALE2) for r in found)
+
+    for dz in range(4):
+        x_first[1, 0, dz].wait_recv()
+
+    def near_x(t, carry):
+        at = t // 3
+        stats_of(lax.rem(i + 3 * at - at // 2, NX), lax.rem(t, 3))
+        return carry
+
+    def far_x(t, carry):
+        stats_of(lax.rem(i + 2, NX), t)
+        return carry
+
+    def far_y(t, carry):
+        stats_of(t, 3)
+        return carry
+
+    lax.fori_loop(0, 9, near_x, 0)
+    for dz in range(4):
+        x_last[0, dz].wait_recv()
+    lax.fori_loop(0, 3, far_x, 0)
     for zc in range(2):
         for way in range(2):
             ring[way, 4, zc, way].wait_recv()
-    first_span = i * (KT // CH)
-
-    def stats_of(x):
-        rows = cols(x, BLOCK)
-        block = jnp.concatenate(
-            [qa[rows, g * WIDTH : (g + 1) * WIDTH] for g in range(GROUP)], axis=0
-        )
-        positions = jnp.concatenate([block_positions(spans, x, j)] * GROUP, axis=1)
-
-        def merge(one, two):
-            top = jnp.maximum(one[0], two[0])
-            return top, one[1] * jnp.exp2((one[0] - top) * SCALE2) + two[1] * jnp.exp2(
-                (two[0] - top) * SCALE2
-            )
-
-        def stats_step(b, carry):
-            following = []
-            for half in range(2):
-                at = 2 * b + half
-                key_block = ka[pl.ds(pl.multiple_of(at * KB, KB), KB), :]
-                starts = [first_span + at * (KB // CH) + n for n in range(KB // CH)]
-                scores = masked_scores(spans, starts, positions, key_block, block)
-                top = jnp.maximum(FLOOR, jnp.max(scores, axis=0, keepdims=True))
-                total = jnp.sum(jnp.exp2((scores - top) * SCALE2), axis=0, keepdims=True)
-                following.append(merge(carry[half], (top, total)))
-            return tuple(following)
-
-        nothing = (
-            jnp.full((1, GROUP * BLOCK), FLOOR, jnp.float32),
-            jnp.zeros((1, GROUP * BLOCK), jnp.float32),
-        )
-        halves = lax.fori_loop(0, KT // KB // 2, stats_step, (nothing, nothing))
-        found = merge(*halves)
-        st[:, rows] = jnp.concatenate(
-            [r[:, g * BLOCK : (g + 1) * BLOCK] for r in found for g in range(GROUP)], axis=0
-        )
-
-    for dz in range(4):
-        x_first[1, 0, dz].wait_recv()
-
-    def early(t, carry):
-        stats_of(lax.rem(i + 3 + t, NX))
-        return carry
-
-    lax.fori_loop(0, 3, early, 0)
-    for dz in range(4):
-        x_last[0, dz].wait_recv()
-    stats_of(lax.rem(i + 2, NX))
+    lax.fori_loop(0, 4, far_y, 0)
     shared = [
         push(st, sa.at[d - 1], send6.at[d], recv6.at[d], x_peer(i, j, h, d)) for d in range(1, NX)
     ]
@@ -323,6 +329,25 @@
     norms = [norm_rows[g : g + 1] for g in range(GROUP)]
 
     query_parts = {}
+
+    def x_to(way):
+        return cols(lax.rem(i + x_ways[way], NX), BLOCK)
+
+    def x_push(src, way, step, g):
+        query_parts[way, step, g] = push(
+            src,
+            rq.at[way, step, g],
+            send8.at[way, step, g],
+            recv8.at[way, step, g],
+            x_peer(i, j, h, x_ways[way]),
+        )
+
+    def x_add(g):
+        way = g // 2
+        query_parts[way, 0, g].wait_recv()
+        total = dq[g, x_to(way), :].astype(jnp.float32) + rq[way, 0, g].astype(jnp.float32)
+        xs[g] = total.astype(jnp.bfloat16)
+        x_push(xs.at[g], way, 1, g)
 
     def grads_of(distances, closing=False):
         owners = [ring_block(j, zc, d) for d in distances for zc in range(2)]
@@ -348,14 +373,9 @@
             )
             if closing:
                 dq[g] = (acc[:, part] + query_term).astype(jnp.bfloat16)
-                for d in range(1, NX):
-                    query_parts[d, g] = push(
-                        dq.at[g, cols(lax.rem(i + d, NX), BLOCK), :],
-                        rq.at[d - 1, g],
-                        send8.at[d, g],
-                        recv8.at[d, g],
-                        x_peer(i, j, h, d),
-                    )
+                way = g // 2
+                x_push(dq.at[g, cols(lax.rem(i + 2, NX), BLOCK), :], way, 0, g)
+                x_push(dq.at[g, x_to(1 - way), :], 1 - way, 1, g)
             else:
                 acc[:, part] += query_term
             key_grad += jnp.dot(score_grads, query_head, preferred_element_type=jnp.float32)
@@ -393,14 +413,13 @@
     for zc in (1, 0):
         for way in range(2):
             back_push(partial[way].at[target(way, 1, zc), :], way, 1, zc, way)
-    for step in (2, 3):
+    for step in range(2, 5):
         for way in range(2):
             grads_of((ways[way] * (5 - step),))
             back_step(way, step)
-    grads_of((1,))
-    back_step(0, 4)
-    grads_of((-1, 0), closing=True)
-    back_step(1, 4)
+    grads_of((0,), closing=True)
+    for g in range(GROUP):
+        x_add(g)
 
     def ring_total(zc, n):
         for way in range(2):
@@ -426,24 +445,24 @@
 
     def give_queries(g):
         total = dq[g, cols(i, BLOCK), :].astype(jnp.float32)
-        for d in range(1, NX):
-            query_parts[d, g].wait_recv()
-            total += rq[d - 1, g].astype(jnp.float32)
+        for way in range(2):
+            query_parts[way, 1, g].wait_recv()
+            total += rq[way, 1, g].astype(jnp.float32)
         sq[g] = total.astype(jnp.bfloat16)
         give(g, sq.at[g], oq.at[:, cols(h * GROUP + g, WIDTH)])
 
-    give_queries(0)
     over = []
     for n in range(2):
         zs[n] = ring_total(1, n).astype(jnp.bfloat16)
         over.append(push(zs.at[n], zr.at[n], send9.at[n], recv9.at[n], z_peer(i, j, h)))
+    give_queries(0)
     give_queries(1)
-    give_queries(2)
     for n, (held, out) in enumerate(((sk, ok), (sv, ov))):
         total = ring_total(0, n)
         over[n].wait_recv()
         held[...] = (total + zr[n].astype(jnp.float32)).astype(jnp.bfloat16)
         give(GROUP + n, held, out.at[:, cols(h, WIDTH)])
+    give_queries(2)
     give_queries(3)
     for copy in kept:
         copy.wait()
@@ -484,7 +503,8 @@
             vmem((GROUP, QT, WIDTH), bf16),
             vmem((KT, WIDTH), bf16),
             vmem((KT, WIDTH), bf16),
-            vmem((NX - 1, GROUP, BLOCK, WIDTH), bf16),
+            vmem((2, 2, GROUP, BLOCK, WIDTH), bf16),
+            vmem((GROUP, BLOCK, WIDTH), bf16),
             vmem((2, 4, 2, 2, BLOCK, WIDTH), bf16),
             vmem((2, 3, 2, 2, BLOCK, WIDTH), bf16),
             vmem((2, BLOCK, WIDTH), bf16),
@@ -501,7 +521,7 @@
         + both(NX)
         + both(NX)
         + both(2, 4, 2, 2)
-        + both(NX, GROUP)
+        + both(2, 2, GROUP)
         + both(2)
         + [dma((GROUP + 2,))]
         + both(HEADS, GROUP + 2),

time: 91.5 us -> 91.2 us (level)
  no operation moved by 1% of the time
where the time goes in v5:
time: 91.2 us; the launch traced here: 91 us
  Pallas kernels  87.4 us (96%)
  local copies, waits for them, and re-layouts  2.96 us (3%)
    pallas_call x1, Pallas kernels, attention(): pl.pallas_call(attention_kernel, out_shape=(jax.ShapeDtypeStruct((OWN, QU...  87.4 us
    unnamed x7, local copies, waits for them, and re-layouts  2.96 us

profile of v5, /device:TPU:1, one launch (start us, length us, event | category | flops | bytes accessed | tf_op | source)
XLA Modules:
  0.0 91.0 jit_solution(3048119339382165519)
XLA Ops:
  0.6 87.4 %attention.1 = (bf16[16,4096]{1,0:T(8,128)(2,1)}, bf16[16,1024]{1,0:T(8,128)(2,1)}, bf16[16,1024]{1,0:T(8,128)(2,1)}) custom-call(s32[128]{0:T(128)} %spans.1, bf16[16,4096]{1,0:T(8,128)(2,1)} %q_ref.1, bf16[16,4096]{1,0:T(8,128)(2,1)} %g_ref.1, bf16[16,1024]{1,0:T(8,128)(2,1)} %k_ref.1, bf16[16,1024]{1,0:T(8,128)(2,1)} %v_ref.1, bf16[16,4096]{1,0:T(8,128)(2,1)} %o_ref.1, ...), custom_call_target="tpu_custom_call" | custom-call | tf_op jit(solution)/shard_map/attention/pallas_call | solution.py:483
  88.0 0.0 copy-start.1
  88.0 1.6 %copy.13 = bf16[16,4096]{1,0:T(8,128)(2,1)} copy(bf16[16,4096]{1,0:T(8,128)(2,1)} %get-tuple-element.6) | data formatting | bytes 262144
  89.6 0.0 copy-done.1
  89.6 0.0 copy-start
  89.6 0.6 copy.14
  90.2 0.2 copy-done
  90.4 0.6 copy.15
Async XLA Ops:
  88.0 1.6 %copy-start.1 = (bf16[16,1024]{1,0:T(8,128)(2,1)S(1)}, bf16[16,1024]{1,0:T(8,128)(2,1)}, u32[]{:S(2)}) copy-start(bf16[16,1024]{1,0:T(8,128)(2,1)} %get-tuple-element.7) | copy-start | bytes 98308
  89.6 0.8 copy-start

commit v6 on v5

--- a/solution.py
+++ b/solution.py
@@ -107,7 +107,7 @@
 
 def attention_kernel(
     spans, q_ref, g_ref, k_ref, v_ref, o_ref, w_ref, oq, ok, ov,
-    e_ref, qa, ga, ka, va, ea, ep, st, sa, acc, dq, dk, dv, rq, xs, rr, run, zs, zr, sq, sk, sv,
+    e_ref, qa, ga, ka, va, ea, ep, st, sa, acc, dq, dk, dv, rq, rr, run, zs, zr, sq, sk, sv,
     local_sem, send1, recv1, send2, recv2, send3, recv3, send4, recv4, send5, recv5,
     send6, recv6, send7, recv7, send8, recv8, send9, recv9, out_sem, send10, recv10,
 ):
@@ -330,25 +330,6 @@
 
     query_parts = {}
 
-    def x_to(way):
-        return cols(lax.rem(i + x_ways[way], NX), BLOCK)
-
-    def x_push(src, way, step, g):
-        query_parts[way, step, g] = push(
-            src,
-            rq.at[way, step, g],
-            send8.at[way, step, g],
-            recv8.at[way, step, g],
-            x_peer(i, j, h, x_ways[way]),
-        )
-
-    def x_add(g):
-        way = g // 2
-        query_parts[way, 0, g].wait_recv()
-        total = dq[g, x_to(way), :].astype(jnp.float32) + rq[way, 0, g].astype(jnp.float32)
-        xs[g] = total.astype(jnp.bfloat16)
-        x_push(xs.at[g], way, 1, g)
-
     def grads_of(distances, closing=False):
         owners = [ring_block(j, zc, d) for d in distances for zc in range(2)]
         rows = [cols(owner, BLOCK) for owner in owners]
@@ -373,9 +354,14 @@
             )
             if closing:
                 dq[g] = (acc[:, part] + query_term).astype(jnp.bfloat16)
-                way = g // 2
-                x_push(dq.at[g, cols(lax.rem(i + 2, NX), BLOCK), :], way, 0, g)
-                x_push(dq.at[g, x_to(1 - way), :], 1 - way, 1, g)
+                for d in range(1, NX):
+                    query_parts[d, g] = push(
+                        dq.at[g, cols(lax.rem(i + d, NX), BLOCK), :],
+                        rq.at[d - 1, g],
+                        send8.at[d, g],
+                        recv8.at[d, g],
+                        x_peer(i, j, h, d),
+                    )
             else:
                 acc[:, part] += query_term
             key_grad += jnp.dot(score_grads, query_head, preferred_element_type=jnp.float32)
@@ -413,13 +399,14 @@
     for zc in (1, 0):
         for way in range(2):
             back_push(partial[way].at[target(way, 1, zc), :], way, 1, zc, way)
-    for step in range(2, 5):
+    for step in (2, 3):
         for way in range(2):
             grads_of((ways[way] * (5 - step),))
             back_step(way, step)
-    grads_of((0,), closing=True)
-    for g in range(GROUP):
-        x_add(g)
+    grads_of((1,))
+    back_step(0, 4)
+    grads_of((-1, 0), closing=True)
+    back_step(1, 4)
 
     def ring_total(zc, n):
         for way in range(2):
@@ -445,24 +432,24 @@
 
     def give_queries(g):
         total = dq[g, cols(i, BLOCK), :].astype(jnp.float32)
-        for way in range(2):
-            query_parts[way, 1, g].wait_recv()
-            total += rq[way, 1, g].astype(jnp.float32)
+        for d in range(1, NX):
+            query_parts[d, g].wait_recv()
+            total += rq[d - 1, g].astype(jnp.float32)
         sq[g] = total.astype(jnp.bfloat16)
         give(g, sq.at[g], oq.at[:, cols(h * GROUP + g, WIDTH)])
 
+    give_queries(0)
     over = []
     for n in range(2):
         zs[n] = ring_total(1, n).astype(jnp.bfloat16)
         over.append(push(zs.at[n], zr.at[n], send9.at[n], recv9.at[n], z_peer(i, j, h)))
-    give_queries(0)
     give_queries(1)
+    give_queries(2)
     for n, (held, out) in enumerate(((sk, ok), (sv, ov))):
         total = ring_total(0, n)
         over[n].wait_recv()
         held[...] = (total + zr[n].astype(jnp.float32)).astype(jnp.bfloat16)
         give(GROUP + n, held, out.at[:, cols(h, WIDTH)])
-    give_queries(2)
     give_queries(3)
     for copy in kept:
         copy.wait()
@@ -503,8 +490,7 @@
             vmem((GROUP, QT, WIDTH), bf16),
             vmem((KT, WIDTH), bf16),
             vmem((KT, WIDTH), bf16),
-            vmem((2, 2, GROUP, BLOCK, WIDTH), bf16),
-            vmem((GROUP, BLOCK, WIDTH), bf16),
+            vmem((NX - 1, GROUP, BLOCK, WIDTH), bf16),
             vmem((2, 4, 2, 2, BLOCK, WIDTH), bf16),
             vmem((2, 3, 2, 2, BLOCK, WIDTH), bf16),
             vmem((2, BLOCK, WIDTH), bf16),
@@ -521,7 +507,7 @@
         + both(NX)
         + both(NX)
         + both(2, 4, 2, 2)
-        + both(2, 2, GROUP)
+        + both(NX, GROUP)
         + both(2)
         + [dma((GROUP + 2,))]
         + both(HEADS, GROUP + 2),

time: 91.2 us -> 90.1 us (0.988)
  Pallas kernels: 87.4 us -> 86.2 us
    pallas_call x1, Pallas kernels: 87.4 us -> 86.2 us  [attention(): pl.pallas_call(attention_kernel, out_shape=(jax.ShapeDtypeStruct((OWN, QU...]
where the time goes in v6:
time: 90.1 us; the launch traced here: 89.8 us
  Pallas kernels  86.2 us (96%)
  local copies, waits for them, and re-layouts  2.96 us (3%)
    pallas_call x1, Pallas kernels, attention(): pl.pallas_call(attention_kernel, out_shape=(jax.ShapeDtypeStruct((OWN, QU...  86.2 us
    unnamed x7, local copies, waits for them, and re-layouts  2.96 us

profile of v6, /device:TPU:1, one launch (start us, length us, event | category | flops | bytes accessed | tf_op | source)
XLA Modules:
  0.0 89.8 jit_solution(5103392630917873868)
XLA Ops:
  0.6 86.2 %attention.1 = (bf16[16,4096]{1,0:T(8,128)(2,1)}, bf16[16,1024]{1,0:T(8,128)(2,1)}, bf16[16,1024]{1,0:T(8,128)(2,1)}) custom-call(s32[128]{0:T(128)} %spans.1, bf16[16,4096]{1,0:T(8,128)(2,1)} %q_ref.1, bf16[16,4096]{1,0:T(8,128)(2,1)} %g_ref.1, bf16[16,1024]{1,0:T(8,128)(2,1)} %k_ref.1, bf16[16,1024]{1,0:T(8,128)(2,1)} %v_ref.1, bf16[16,4096]{1,0:T(8,128)(2,1)} %o_ref.1, ...), custom_call_target="tpu_custom_call" | custom-call | tf_op jit(solution)/shard_map/attention/pallas_call | solution.py:470
  86.9 0.0 copy-start.1
  86.9 1.6 %copy.13 = bf16[16,4096]{1,0:T(8,128)(2,1)} copy(bf16[16,4096]{1,0:T(8,128)(2,1)} %get-tuple-element.6) | data formatting | bytes 262144
  88.4 0.0 copy-done.1
  88.4 0.0 copy-start
  88.4 0.6 copy.14
  89.1 0.2 copy-done
  89.2 0.6 copy.15
Async XLA Ops:
  86.9 1.6 %copy-start.1 = (bf16[16,1024]{1,0:T(8,128)(2,1)S(1)}, bf16[16,1024]{1,0:T(8,128)(2,1)}, u32[]{:S(2)}) copy-start(bf16[16,1024]{1,0:T(8,128)(2,1)} %get-tuple-element.7) | copy-start | bytes 98308
  88.4 0.8 copy-start
